TPU v7x, 32 devices: a whole 2x2x4 slice. The times are simulated.
32 devices in a mesh: gen: 4 (over y, x), dom: 4 (over z), dp: 2 (over core).
Axes of the slice: x: 2, y: 2, z: 4, core: 2. Of those that a mesh axis runs over, the one named last changes fastest.
Arguments:
- gen_hidden: bfloat16 [1024, 4096], P(('dp', 'dom'), 'gen'), parts along dimension 0, may hold values from -52 to 52
- gen_gain: float32 [8192], P('dp'), parts along dimension 0, may hold values from 0.25 to 1.75
- gen_head: bfloat16 [131072, 4096], P(('dp', 'gen', 'dom')), parts along dimension 0, may hold values from -24 to 24
- dom_hidden: bfloat16 [1024, 4096], P(('dp', 'gen'), 'dom'), parts along dimension 0, may hold values from -52 to 52
- dom_gain: float32 [8192], P('dp'), parts along dimension 0, may hold values from 0.25 to 1.75
- dom_head: bfloat16 [131072, 4096], P(('dp', 'gen', 'dom')), parts along dimension 0, may hold values from -24 to 24
- targets: int32 [1024], P('dp'), parts along dimension 0, may hold values from 0 to 65535
- doc_ids: int32 [1024], P('dp'), parts along dimension 0, may hold values from -1 to 31, as said below
Outputs:
- token_diff: float32 [1024], P(('dp', 'dom')), parts along dimension 0
- doc_score: float32 [64], P(('dp', 'dom')), parts along dimension 0
There are 2 independent parts, one for each index of `dp`. A program takes and returns all parts, laid end to end along the dimension named above; each array names one. Nothing has to cross between parts.
Inputs may be any that keep to these rules, and one draw needn't show every extreme that they name: `doc_ids`: rows 128 * p to 128 * p + 127 form pack p. Each pack begins with rows of exactly 8 documents, numbered 8 * p onwards in order, each one row or more, and ends with padding rows marked -1. The packs fall into pairs whose document rows add up to 136, so the batch holds 272 document rows, and some pack has no padding.
All inputs are finite; a program needn't handle non-finite values.
Results may differ from a plain program's by a relative error of at most 0.0045.
Values may be sent and summed in bfloat16 or wider, within the bound.
No kernel may reach another device: no remote copies, remote signals or barrier semaphores. Data moves between devices by JAX's collectives and lax.ppermute only.
A program may use at most 128 MiB of HBM per device.

v0:
```python
import functools

import jax
import jax.numpy as jnp
from jax import lax
from jax.experimental import pallas as pl
from jax.experimental.pallas import tpu as pltpu
from jax.sharding import PartitionSpec as P


DOC_PACK = 8
EPS = 1e-05
HALVES = 2
VMEM = pltpu.VMEM
SMEM = pltpu.SMEM


def whole(memory_space=VMEM):
    return pl.BlockSpec(memory_space=memory_space)


def origin(axis, index, k, count):
    if axis == "gen" and count & (count - 1) == 0:
        return index ^ k
    return (index - k + count) % count


def around(block, axis):
    count = lax.axis_size(axis)
    parts = [block]
    for k in range(1, count):
        pairs = [(origin(axis, i, k, count), i) for i in range(count)]
        parts.append(lax.ppermute(block, axis, pairs))
    return parts


def pack_extents(doc):
    live = jnp.where(doc >= 0, 1.0, 0.0)
    counts = jnp.sum(live, axis=1, keepdims=True)
    ahead = jnp.zeros((1, 1), jnp.float32)
    extents = []
    for p in range(doc.shape[0]):
        count = counts[p : p + 1, :]
        extents.append((count, ahead))
        ahead = ahead + count
    return extents


def slot_mask(extent, slots, rows):
    count, ahead = extent
    slot = lax.broadcasted_iota(jnp.int32, (slots, rows), 0).astype(jnp.float32)
    row = lax.broadcasted_iota(jnp.int32, (slots, rows), 1).astype(jnp.float32)
    return (slot - ahead == row) & (row < count)


def compact_kernel(pack_axis, spans, index_ref, doc_ref, *refs):
    part_refs = refs[:-2] if spans else refs[:-1]
    out_ref = refs[len(part_refs)]
    packs, rows = doc_ref.shape
    slots = out_ref.shape[0]
    extents = pack_extents(doc_ref[...])
    mine = index_ref[0]
    total = None
    for k, part_ref in enumerate(part_refs):
        pack = origin(pack_axis, mine, k, packs)
        count = jnp.zeros((1, 1), jnp.float32)
        ahead = jnp.zeros((1, 1), jnp.float32)
        for p in range(packs):
            here = jnp.where(pack == p, 1.0, 0.0)
            count = count + extents[p][0] * here
            ahead = ahead + extents[p][1] * here
        mask = slot_mask((count, ahead), slots, rows)
        onehot = jnp.where(mask, 1.0, 0.0).astype(jnp.bfloat16)
        piece = jnp.dot(onehot, part_ref[...], preferred_element_type=jnp.float32)
        total = piece if total is None else total + piece
    out_ref[...] = total.astype(jnp.bfloat16)
    if spans:
        span_ref = refs[-1]
        width = span_ref.shape[1]
        start = pl.multiple_of(lax.rem(mine, spans) * width, width)
        span_ref[...] = out_ref[:, pl.ds(start, width)]


def compact(parts, doc, index, slots, pack_axis, spans=0):
    width = parts[0].shape[1]
    out_shape = [jax.ShapeDtypeStruct((slots, width), jnp.bfloat16)]
    if spans:
        out_shape.append(jax.ShapeDtypeStruct((slots, width // spans), jnp.bfloat16))
    return pl.pallas_call(
        functools.partial(compact_kernel, pack_axis, spans),
        out_shape=out_shape,
        in_specs=[whole(SMEM), whole()] + [whole() for _ in parts],
        out_specs=[whole()] * len(out_shape),
        compiler_params=pltpu.CompilerParams(vmem_limit_bytes=16 * 1024 * 1024),
        cost_estimate=pl.CostEstimate(
            flops=2 * slots * width * doc.size,
            bytes_accessed=2 * width * (doc.size + slots),
            transcendentals=0,
        ),
    )(index, doc, *parts)


def tally(logits, wanted, top, total, picked):
    lanes = top.shape[1]
    groups = [logits[:, at : at + lanes] for at in range(0, logits.shape[1], lanes)]
    former = top[...]
    highest = functools.reduce(jnp.maximum, groups, former)
    lane = lax.broadcasted_iota(jnp.int32, former.shape, 1)
    away = wanted - lane
    latest = total[...] * jnp.exp(former - highest)
    hit = picked[...]
    for k, group in enumerate(groups):
        latest = latest + jnp.exp(group - highest)
        hit = jnp.where(away == k * lanes, group, hit)
    top[...] = highest
    total[...] = latest
    picked[...] = hit


def summed_up(top, total, picked):
    highest = jnp.max(top[...], axis=1, keepdims=True)
    everything = jnp.sum(total[...] * jnp.exp(top[...] - highest), axis=1, keepdims=True)
    return highest + jnp.log(everything), jnp.sum(picked[...], axis=1, keepdims=True)


def stats_kernel(pieces, buffers, index_ref, doc_ref, target_ref, gain_ref, head_ref, *refs):
    part_count = pieces[-1][0] + 1
    part_refs = refs[:part_count]
    out_ref, normed, tiles, sems, top, total, picked, wanted = refs[part_count:]
    slots, width = normed.shape
    tile = tiles.shape[1]
    packs, rows = doc_ref.shape
    j = pl.program_id(0)
    steps = pl.num_programs(0)

    def copy(step):
        slot = lax.rem(step, buffers)
        return pltpu.make_async_copy(
            head_ref.at[pl.ds(pl.multiple_of(step * tile, tile), tile), :],
            tiles.at[slot],
            sems.at[slot],
        )

    @pl.when(j == 0)
    def _():
        copy(0).start()
        for step in range(1, buffers - 1):
            pl.when(step < steps)(lambda: copy(step).start())

    @pl.when(j + buffers - 1 < steps)
    def _():
        copy(j + buffers - 1).start()

    @pl.when(j == 0)
    def _():
        sums = jnp.zeros((slots, 1), jnp.float32)
        for part_ref in part_refs:
            values = part_ref[...].astype(jnp.float32)
            sums = sums + jnp.sum(values * values, axis=1, keepdims=True)
        scale = lax.rsqrt(sums / width + EPS)
        for k, (part, start, extent) in enumerate(pieces):
            at = pl.ds(pl.multiple_of(index_ref[k], 128), extent)
            values = part_refs[part][:, start : start + extent].astype(jnp.float32)
            normed[:, at] = (values * scale * gain_ref[:, at]).astype(jnp.bfloat16)
        extents = pack_extents(doc_ref[...])
        ids = jnp.zeros((slots, 1), jnp.float32)
        for p in range(packs):
            mask = slot_mask(extents[p], slots, rows)
            row = (target_ref[p : p + 1, :] - index_ref[len(pieces)]).astype(jnp.float32)
            ids = ids + jnp.sum(jnp.where(mask, row, 0.0), axis=1, keepdims=True)
        wanted[...] = jnp.broadcast_to(ids.astype(jnp.int32), wanted.shape)
        top[...] = jnp.full(top.shape, -jnp.inf, jnp.float32)
        total[...] = jnp.zeros(total.shape, jnp.float32)
        picked[...] = jnp.zeros(picked.shape, jnp.float32)

    copy(j).wait()
    logits = lax.dot_general(
        normed[...],
        tiles[lax.rem(j, buffers)],
        (((1,), (1,)), ((), ())),
        preferred_element_type=jnp.float32,
    )
    tally(logits, wanted[...] - j * tile, top, total, picked)

    @pl.when(j == steps - 1)
    def _():
        log_total, logit = summed_up(top, total, picked)
        extents = pack_extents(doc_ref[...])
        for p in range(packs):
            mask = slot_mask(extents[p], slots, rows)
            out_ref[p, 0:1, :] = jnp.sum(jnp.where(mask, log_total, 0.0), axis=0, keepdims=True)
            out_ref[p, 1:2, :] = jnp.sum(jnp.where(mask, logit, 0.0), axis=0, keepdims=True)


def stats(parts, first, gain, head, doc, target):
    slots = parts[0][0].shape[0]
    vocab, width = head.shape
    packs, rows = doc.shape
    tile = min(512, vocab)
    buffers = 3
    pieces, starts = [], []
    for number, (array, places) in enumerate(parts):
        extent = array.shape[1] // len(places)
        for k, place in enumerate(places):
            pieces.append((number, k * extent, extent))
            starts.append(place)
    index = jnp.stack(starts + [first]).astype(jnp.int32)
    column = VMEM((slots, 128), jnp.float32)
    return pl.pallas_call(
        functools.partial(stats_kernel, tuple(pieces), buffers),
        grid=(vocab // tile,),
        in_specs=[whole(SMEM), whole(), whole(), whole(), whole(pl.ANY)] + [whole() for _ in parts],
        out_specs=whole(),
        out_shape=jax.ShapeDtypeStruct((packs, 2, rows), jnp.float32),
        scratch_shapes=[
            VMEM((slots, width), jnp.bfloat16),
            VMEM((buffers, tile, width), jnp.bfloat16),
            pltpu.SemaphoreType.DMA((buffers,)),
            column,
            column,
            column,
            VMEM((slots, 128), jnp.int32),
        ],
        compiler_params=pltpu.CompilerParams(vmem_limit_bytes=32 * 1024 * 1024),
        cost_estimate=pl.CostEstimate(
            flops=2 * slots * width * vocab,
            bytes_accessed=2 * width * (vocab + slots),
            transcendentals=slots * vocab,
        ),
    )(index, doc, target, gain.reshape(1, width), head, *[array for array, _ in parts])


def finish_kernel(index_ref, doc_ref, all_ref, token_ref, score_ref):
    pack = index_ref[0]
    members = all_ref.shape[0]
    both = all_ref[...]

    def log_prob(at):
        logs = [both[i, at : at + 1, :] for i in range(members)]
        highest = functools.reduce(jnp.maximum, logs)
        summed = functools.reduce(jnp.add, [jnp.exp(one - highest) for one in logs])
        logit = functools.reduce(jnp.add, [both[i, at + 1 : at + 2, :] for i in range(members)])
        return logit - (highest + jnp.log(summed))

    ids = doc_ref[pl.ds(pack, 1), :]
    diff = jnp.where(ids >= 0, log_prob(2) - log_prob(0), 0.0)
    token_ref[...] = diff
    rows = ids.shape[1]
    number = lax.broadcasted_iota(jnp.int32, (DOC_PACK, rows), 0) + pack * DOC_PACK
    mine = number == ids
    sums = jnp.sum(jnp.where(mine, diff, 0.0), axis=1, keepdims=True)
    counts = jnp.sum(jnp.where(mine, 1.0, 0.0), axis=1, keepdims=True)
    score = sums / counts
    row = lax.broadcasted_iota(jnp.int32, (DOC_PACK, DOC_PACK), 0)
    column = lax.broadcasted_iota(jnp.int32, (DOC_PACK, DOC_PACK), 1)
    score_ref[...] = jnp.sum(jnp.where(row == column, score, 0.0), axis=0, keepdims=True)


def finish(gathered, doc, index):
    rows = doc.shape[1]
    token, score = pl.pallas_call(
        finish_kernel,
        out_shape=(
            jax.ShapeDtypeStruct((1, rows), jnp.float32),
            jax.ShapeDtypeStruct((1, DOC_PACK), jnp.float32),
        ),
        in_specs=[whole(SMEM), whole(), whole()],
        out_specs=(whole(), whole()),
    )(index, doc, gathered)
    return token.reshape(rows), score.reshape(DOC_PACK)


def per_device(gen_hidden, gen_gain, gen_head, dom_hidden, dom_gain, dom_head, targets, doc_ids):
    rows = gen_hidden.shape[0]
    gen_count = lax.axis_size("gen")
    dom_count = lax.axis_size("dom")
    gen_index = lax.axis_index("gen")
    dom_index = lax.axis_index("dom")
    first = (gen_index * dom_count + dom_index) * gen_head.shape[0]
    gen_at = jnp.stack([gen_index, first]).astype(jnp.int32)
    dom_at = jnp.stack([dom_index, first]).astype(jnp.int32)
    doc = doc_ids.reshape(dom_count, rows)
    target = targets.reshape(dom_count, rows)
    slots = dom_count // 2 * (rows + DOC_PACK)

    block_width = gen_hidden.shape[1]
    half = block_width // HALVES
    dom_width = dom_hidden.shape[1]
    spans = gen_count if dom_width % (gen_count * 128) == 0 else 0
    gen_first = [around(gen_hidden[:, h * half : (h + 1) * half], "dom") for h in range(HALVES)]
    dom_first = around(dom_hidden, "gen")
    gen_parts = []
    for h in range(HALVES):
        (rows_in,) = compact(gen_first[h], doc, dom_at, slots, "dom")
        for k, part in enumerate(around(rows_in, "gen")):
            place = origin("gen", gen_index, k, gen_count) * block_width + h * half
            gen_parts.append((part, [place]))
    dom_rows, *dom_span = compact(dom_first, doc, gen_at, slots, "gen", spans)
    places = [origin("dom", dom_index, k, dom_count) * dom_width for k in range(dom_count)]
    dom_parts = [(dom_rows, places[:1])]
    if spans:
        span = dom_width // spans
        received = around(dom_span[0], "dom")[1:]
        joined = jnp.concatenate(received, axis=1)
        for k, part in enumerate(around(joined, "gen")):
            at = origin("gen", gen_index, k, gen_count) * span
            dom_parts.append((part, [place + at for place in places[1:]]))
    else:
        for k, part in enumerate(around(dom_rows, "dom")[1:]):
            dom_parts.append((part, places[k + 1 : k + 2]))
    gen_stats = stats(gen_parts, first, gen_gain, gen_head, doc, target)
    dom_stats = stats(dom_parts, first, dom_gain, dom_head, doc, target)
    both = jnp.concatenate([gen_stats, dom_stats], axis=1)
    sent = jnp.broadcast_to(both[None], (gen_count,) + both.shape)
    sent = sent.reshape((gen_count * dom_count,) + both.shape[1:])
    gathered = lax.all_to_all(sent, ("gen", "dom"), 0, 0)
    return finish(gathered, doc, dom_at)


def solution(mesh):
    in_specs = (
        P(("dp", "dom"), "gen"),
        P("dp"),
        P(("dp", "gen", "dom"), None),
        P(("dp", "gen"), "dom"),
        P("dp"),
        P(("dp", "gen", "dom"), None),
        P("dp"),
        P("dp"),
    )
    out_specs = (P(("dp", "dom")), P(("dp", "dom")))
    return jax.shard_map(
        per_device, mesh=mesh, in_specs=in_specs, out_specs=out_specs, check_vma=False
    )
```

profile of v0, /device:TPU:0, one launch (start us, length us, event | category | flops | bytes accessed | tf_op | source)
XLA Modules:
  0.0 107.7 jit_solution(13031103117005938336)
XLA Ops:
  0.6 0.0 copy-start.7
  0.6 0.0 copy-start.5
  0.7 1.0 fusion
  1.7 3.1 %collective-permute-start = (bf16[128,512]{1,0:T(8,128)(2,1)S(1)}, bf16[128,512]{1,0:T(8,128)(2,1)S(1)}, u32[]{:S(2)}, u32[]{:S(2)}) collective-permute-start(bf16[128,512]{1,0:T(8,128)(2,1)S(1)} %get-tuple-element.11.refs_0_), channel_id=1, source_target_pairs={{6,0},{0,2},{2,4},{4,6},{7,1},{1,3},{3,5},{5,7},{14,8},{8,10},{10,... | collective-permute-start | bytes 393224 | tf_op jit(solution)/shard_map/ppermute | solution.py:33
  4.8 1.5 %collective-permute-start.12 = (bf16[128,1024]{1,0:T(8,128)(2,1)}, bf16[128,1024]{1,0:T(8,128)(2,1)S(1)}, u32[]{:S(2)}, u32[]{:S(2)}) collective-permute-start(bf16[128,1024]{1,0:T(8,128)(2,1)} %refs_0_.1), channel_id=1, source_target_pairs={{8,0},{0,8},{24,16},{16,24},{9,1},{1,9},{25,17},{17,25},{10,2},{2,... | collective-permute-start | bytes 786440 | tf_op jit(solution)/shard_map/ppermute | solution.py:33
  6.2 1.5 %collective-permute-start.13 = (bf16[128,1024]{1,0:T(8,128)(2,1)}, bf16[128,1024]{1,0:T(8,128)(2,1)S(1)}, u32[]{:S(2)}, u32[]{:S(2)}) collective-permute-start(bf16[128,1024]{1,0:T(8,128)(2,1)} %refs_0_.1), channel_id=1, source_target_pairs={{16,0},{24,8},{0,16},{8,24},{17,1},{25,9},{1,17},{9,25},{18,2},{26... | collective-permute-start | bytes 786440 | tf_op jit(solution)/shard_map/ppermute | solution.py:33
  7.8 0.5 collective-permute-start.14
  8.2 2.6 %collective-permute-start.1 = (bf16[128,512]{1,0:T(8,128)(2,1)S(1)}, bf16[128,512]{1,0:T(8,128)(2,1)S(1)}, u32[]{:S(2)}, u32[]{:S(2)}) collective-permute-start(bf16[128,512]{1,0:T(8,128)(2,1)S(1)} %get-tuple-element.11.refs_0_), channel_id=1, source_target_pairs={{4,0},{6,2},{0,4},{2,6},{5,1},{7,3},{1,5},{3,7},{12,8},{14,10},{8,... | collective-permute-start | bytes 393224 | tf_op jit(solution)/shard_map/ppermute | solution.py:33
  10.8 0.0 collective-permute-done.refs_1_
  10.8 1.3 %collective-permute-start.2 = (bf16[128,512]{1,0:T(8,128)(2,1)S(1)}, bf16[128,512]{1,0:T(8,128)(2,1)S(1)}, u32[]{:S(2)}, u32[]{:S(2)}) collective-permute-start(bf16[128,512]{1,0:T(8,128)(2,1)S(1)} %get-tuple-element.11.refs_0_), channel_id=1, source_target_pairs={{2,0},{4,2},{6,4},{0,6},{3,1},{5,3},{7,5},{1,7},{10,8},{12,10},{14... | collective-permute-start | bytes 393224 | tf_op jit(solution)/shard_map/ppermute | solution.py:33
  12.2 0.1 pad_add_fusion.index_ref
  12.3 4.9 %collective-permute-done.1.refs_2_ = bf16[128,512]{1,0:T(8,128)(2,1)S(1)} collective-permute-done((bf16[128,512]{1,0:T(8,128)(2,1)S(1)}, bf16[128,512]{1,0:T(8,128)(2,1)S(1)}, u32[]{:S(2)}, u32[]{:S(2)}) %collective-permute-start.1) | collective-permute-done | bytes 131104 | tf_op jit(solution)/shard_map/ppermute | solution.py:33
  17.2 2.5 %collective-permute-start.6 = (bf16[128,512]{1,0:T(8,128)(2,1)S(1)}, bf16[128,512]{1,0:T(8,128)(2,1)S(1)}, u32[]{:S(2)}, u32[]{:S(2)}) collective-permute-start(bf16[128,512]{1,0:T(8,128)(2,1)S(1)} %get-tuple-element.10.refs_0_), channel_id=1, source_target_pairs={{6,0},{0,2},{2,4},{4,6},{7,1},{1,3},{3,5},{5,7},{14,8},{8,10},{10,... | collective-permute-start | bytes 393224 | tf_op jit(solution)/shard_map/ppermute | solution.py:33
  19.6 0.0 collective-permute-done.2.refs_3_
  19.7 3.4 %collective-permute-start.7 = (bf16[128,512]{1,0:T(8,128)(2,1)S(1)}, bf16[128,512]{1,0:T(8,128)(2,1)S(1)}, u32[]{:S(2)}, u32[]{:S(2)}) collective-permute-start(bf16[128,512]{1,0:T(8,128)(2,1)S(1)} %get-tuple-element.10.refs_0_), channel_id=1, source_target_pairs={{4,0},{6,2},{0,4},{2,6},{5,1},{7,3},{1,5},{3,7},{12,8},{14,10},{8,... | collective-permute-start | bytes 393224 | tf_op jit(solution)/shard_map/ppermute | solution.py:33
  23.0 0.7 copy-done
  23.7 1.1 %shard_map.95.refs_0_ = bf16[272,512]{1,0:T(8,128)(2,1)S(1)} custom-call(s32[2]{0:T(128)S(1)} %pad_add_fusion.index_ref, s32[4,128]{1,0:T(4,128)S(1)} %bitcast.32, bf16[128,512]{1,0:T(8,128)(2,1)S(1)} %get-tuple-element.11.refs_0_, bf16[128,512]{1,0:T(8,128)(2,1)S(1)} %collective-permute-done.refs_1_, bf16[128,512]{1,0:T(8,128)(2,1)S(1)} %collective-permute-done.1.refs_2_, ...), custom_call_target="tpu_custom_call" | custom-call | flops 142606336 | bytes 802816 | tf_op jit(solution)/shard_map/pallas_call | solution.py:89
  24.8 0.0 collective-permute-done.12.refs_1_
  24.8 1.6 %collective-permute-start.3 = (bf16[272,512]{1,0:T(8,128)(2,1)S(1)}, bf16[272,512]{1,0:T(8,128)(2,1)S(1)}, u32[]{:S(2)}, u32[]{:S(2)}) collective-permute-start(bf16[272,512]{1,0:T(8,128)(2,1)S(1)} %shard_map.95.refs_0_), channel_id=1, source_target_pairs={{8,0},{0,8},{24,16},{16,24},{9,1},{1,9},{25,17},{17,25},{10,2},{2,... | collective-permute-start | bytes 835592 | tf_op jit(solution)/shard_map/ppermute | solution.py:33
  26.4 0.1 pad_add_fusion.1.index_ref
  26.5 0.0 collective-permute-done.13.refs_2_
  26.5 0.0 collective-permute-start.8
  26.5 0.0 collective-permute-done.14.refs_3_
  26.5 0.0 copy-start.1
  26.5 0.7 copy-done.1
  27.2 0.9 copy-done.9
  28.1 1.4 %shard_map.98 = (bf16[272,1024]{1,0:T(8,128)(2,1)S(1)}, bf16[272,256]{1,0:T(8,128)(2,1)S(1)}) custom-call(s32[2]{0:T(128)S(1)} %pad_add_fusion.1.index_ref, s32[4,128]{1,0:T(4,128)S(1)} %bitcast.33, bf16[128,1024]{1,0:T(8,128)(2,1)S(1)} %copy-done.9, bf16[128,1024]{1,0:T(8,128)(2,1)S(1)} %collective-permute-done.12.refs_1_, ...), custom_call_target="tpu_custom_call" | custom-call | flops 285212672 | bytes 1605632 | tf_op jit(solution)/shard_map/pallas_call | solution.py:89
  29.5 2.1 %collective-permute-start.15 = (bf16[272,256]{1,0:T(8,128)(2,1)S(1)}, bf16[272,256]{1,0:T(8,128)(2,1)S(1)}, u32[]{:S(2)}, u32[]{:S(2)}) collective-permute-start(bf16[272,256]{1,0:T(8,128)(2,1)S(1)} %get-tuple-element.7), channel_id=1, source_target_pairs={{6,0},{0,2},{2,4},{4,6},{7,1},{1,3},{3,5},{5,7},{14,8},{8,10},{10,... | collective-permute-start | bytes 417800 | tf_op jit(solution)/shard_map/ppermute | solution.py:33
  31.6 0.0 collective-permute-done.6.refs_1_
  31.6 0.0 collective-permute-start.16
  31.6 0.0 collective-permute-done.7.refs_2_
  31.6 2.4 %collective-permute-start.17 = (bf16[272,256]{1,0:T(8,128)(2,1)S(1)}, bf16[272,256]{1,0:T(8,128)(2,1)S(1)}, u32[]{:S(2)}, u32[]{:S(2)}) collective-permute-start(bf16[272,256]{1,0:T(8,128)(2,1)S(1)} %get-tuple-element.7), channel_id=1, source_target_pairs={{2,0},{4,2},{6,4},{0,6},{3,1},{5,3},{7,5},{1,7},{10,8},{12,10},{14... | collective-permute-start | bytes 417800 | tf_op jit(solution)/shard_map/ppermute | solution.py:33
  34.0 0.1 stack.98.index_ref
  34.1 0.1 stack.112.index_ref
  34.2 0.0 collective-permute-done.8.refs_3_
  34.2 1.6 %collective-permute-start.4 = (bf16[272,512]{1,0:T(8,128)(2,1)S(1)}, bf16[272,512]{1,0:T(8,128)(2,1)S(1)}, u32[]{:S(2)}, u32[]{:S(2)}) collective-permute-start(bf16[272,512]{1,0:T(8,128)(2,1)S(1)} %shard_map.95.refs_0_), channel_id=1, source_target_pairs={{16,0},{24,8},{0,16},{8,24},{17,1},{25,9},{1,17},{9,25},{18,2},{26... | collective-permute-start | bytes 835592 | tf_op jit(solution)/shard_map/ppermute | solution.py:33
  35.8 0.7 copy-done.2
  36.5 1.1 %shard_map.96.refs_4_ = bf16[272,512]{1,0:T(8,128)(2,1)S(1)} custom-call(s32[2]{0:T(128)S(1)} %pad_add_fusion.index_ref, s32[4,128]{1,0:T(4,128)S(1)} %bitcast.34, bf16[128,512]{1,0:T(8,128)(2,1)S(1)} %get-tuple-element.10.refs_0_, bf16[128,512]{1,0:T(8,128)(2,1)S(1)} %collective-permute-done.6.refs_1_, bf16[128,512]{1,0:T(8,128)(2,1)S(1)} %collective-permute-done.7.refs_2_, ...), custom_call_target="tpu_custom_call" | custom-call | flops 142606336 | bytes 802816 | tf_op jit(solution)/shard_map/pallas_call | solution.py:89
  37.6 0.0 collective-permute-done.15
  37.6 3.9 %collective-permute-start.5 = (bf16[272,512]{1,0:T(8,128)(2,1)S(1)}, bf16[272,512]{1,0:T(8,128)(2,1)S(1)}, u32[]{:S(2)}, u32[]{:S(2)}) collective-permute-start(bf16[272,512]{1,0:T(8,128)(2,1)S(1)} %shard_map.95.refs_0_), channel_id=1, source_target_pairs={{24,0},{16,8},{8,16},{0,24},{25,1},{17,9},{9,17},{1,25},{26,2},{18... | collective-permute-start | bytes 835592 | tf_op jit(solution)/shard_map/ppermute | solution.py:33
  41.5 0.0 collective-permute-done.16
  41.5 1.6 %collective-permute-start.9 = (bf16[272,512]{1,0:T(8,128)(2,1)S(1)}, bf16[272,512]{1,0:T(8,128)(2,1)S(1)}, u32[]{:S(2)}, u32[]{:S(2)}) collective-permute-start(bf16[272,512]{1,0:T(8,128)(2,1)S(1)} %shard_map.96.refs_4_), channel_id=1, source_target_pairs={{8,0},{0,8},{24,16},{16,24},{9,1},{1,9},{25,17},{17,25},{10,2},{2,... | collective-permute-start | bytes 835592 | tf_op jit(solution)/shard_map/ppermute | solution.py:33
  43.2 0.0 collective-permute-done.17
  43.2 1.5 %collective-permute-start.10 = (bf16[272,512]{1,0:T(8,128)(2,1)S(1)}, bf16[272,512]{1,0:T(8,128)(2,1)S(1)}, u32[]{:S(2)}, u32[]{:S(2)}) collective-permute-start(bf16[272,512]{1,0:T(8,128)(2,1)S(1)} %shard_map.96.refs_4_), channel_id=1, source_target_pairs={{16,0},{24,8},{0,16},{8,24},{17,1},{25,9},{1,17},{9,25},{18,2},{26... | collective-permute-start | bytes 835592 | tf_op jit(solution)/shard_map/ppermute | solution.py:33
  44.7 0.0 collective-permute-done.3.refs_1_
  44.7 0.4 collective-permute-start.11
  45.1 0.0 collective-permute-done.4.refs_2_
  45.1 1.7 %collective-permute-start.18 = (bf16[272,768]{1,0:T(8,128)(2,1)S(1)}, bf16[272,768]{1,0:T(8,128)(2,1)S(1)}, u32[]{:S(2)}, u32[]{:S(2)}) collective-permute-start(bf16[272,768]{1,0:T(8,128)(2,1)S(1)} %constant_dynamic-update-slice_fusion.refs_1_), channel_id=1, source_target_pairs={{8,0},{0,8},{24,16},{16,24},{9,1},{1,9},{25,17},{17,25},{10,2},{2,... | collective-permute-start | bytes 1253384 | tf_op jit(solution)/shard_map/ppermute | solution.py:33
  46.8 2.4 %collective-permute-done.5.refs_3_ = bf16[272,512]{1,0:T(8,128)(2,1)S(1)} collective-permute-done((bf16[272,512]{1,0:T(8,128)(2,1)S(1)}, bf16[272,512]{1,0:T(8,128)(2,1)S(1)}, u32[]{:S(2)}, u32[]{:S(2)}) %collective-permute-start.5) | collective-permute-done | bytes 278560 | tf_op jit(solution)/shard_map/ppermute | solution.py:33
  49.1 1.5 %collective-permute-start.19 = (bf16[272,768]{1,0:T(8,128)(2,1)S(1)}, bf16[272,768]{1,0:T(8,128)(2,1)S(1)}, u32[]{:S(2)}, u32[]{:S(2)}) collective-permute-start(bf16[272,768]{1,0:T(8,128)(2,1)S(1)} %constant_dynamic-update-slice_fusion.refs_1_), channel_id=1, source_target_pairs={{16,0},{24,8},{0,16},{8,24},{17,1},{25,9},{1,17},{9,25},{18,2},{26... | collective-permute-start | bytes 1253384 | tf_op jit(solution)/shard_map/ppermute | solution.py:33
  50.6 4.5 %collective-permute-done.9.refs_5_ = bf16[272,512]{1,0:T(8,128)(2,1)S(1)} collective-permute-done((bf16[272,512]{1,0:T(8,128)(2,1)S(1)}, bf16[272,512]{1,0:T(8,128)(2,1)S(1)}, u32[]{:S(2)}, u32[]{:S(2)}) %collective-permute-start.9) | collective-permute-done | bytes 278560 | tf_op jit(solution)/shard_map/ppermute | solution.py:33
  55.1 2.9 %collective-permute-start.20 = (bf16[272,768]{1,0:T(8,128)(2,1)S(1)}, bf16[272,768]{1,0:T(8,128)(2,1)S(1)}, u32[]{:S(2)}, u32[]{:S(2)}) collective-permute-start(bf16[272,768]{1,0:T(8,128)(2,1)S(1)} %constant_dynamic-update-slice_fusion.refs_1_), channel_id=1, source_target_pairs={{24,0},{16,8},{8,16},{0,24},{25,1},{17,9},{9,17},{1,25},{26,2},{18... | collective-permute-start | bytes 1253384 | tf_op jit(solution)/shard_map/ppermute | solution.py:33
  58.0 0.6 collective-permute-done.10.refs_6_
  58.7 2.3 %collective-permute-done.11.refs_7_ = bf16[272,512]{1,0:T(8,128)(2,1)S(1)} collective-permute-done((bf16[272,512]{1,0:T(8,128)(2,1)S(1)}, bf16[272,512]{1,0:T(8,128)(2,1)S(1)}, u32[]{:S(2)}, u32[]{:S(2)}) %collective-permute-start.11) | collective-permute-done | bytes 278560 | tf_op jit(solution)/shard_map/ppermute | solution.py:33
  61.0 0.7 copy-done.3
  61.7 0.7 copy-done.4
  62.4 0.7 copy-done.6
  63.1 14.8 %shard_map.97 = f32[4,2,128]{2,1,0:T(2,128)S(1)} custom-call(s32[9]{0:T(128)S(1)} %stack.98.index_ref, s32[4,128]{1,0:T(4,128)S(1)} %bitcast.35, s32[4,128]{1,0:T(4,128)S(1)} %bitcast.39, f32[1,4096]{1,0:T(1,128)S(1)} %bitcast.37, bf16[4096,4096]{1,0:T(8,128)(2,1)} %head_ref.2, bf16[272,512]{1,0:T(8,128)(2,1)S(1)} %shard_map.95.refs_0_, ...), custom_call_target="tpu_custom_call" | custom-call | flops 9126805504 | bytes 35782656 | tf_op jit(solution)/shard_map/pallas_call | solution.py:209
  77.9 0.0 collective-permute-done.18.refs_2_
  77.9 0.0 collective-permute-done.19.refs_3_
  77.9 0.0 collective-permute-done.20.refs_4_
  78.0 14.9 %shard_map.99 = f32[4,2,128]{2,1,0:T(2,128)S(1)} custom-call(s32[14]{0:T(128)S(1)} %stack.112.index_ref, s32[4,128]{1,0:T(4,128)S(1)} %bitcast.36, s32[4,128]{1,0:T(4,128)S(1)} %bitcast.40, f32[1,4096]{1,0:T(1,128)S(1)} %bitcast.38, bf16[4096,4096]{1,0:T(8,128)(2,1)} %head_ref.3, bf16[272,1024]{1,0:T(8,128)(2,1)S(1)} %get-tuple-element.6.refs_0_, ...), custom_call_target="tpu_custom_call" | custom-call | flops 9126805504 | bytes 35782656 | tf_op jit(solution)/shard_map/pallas_call | solution.py:209
  92.9 13.4 %all_to_all.5.all_ref = f32[16,4,128]{2,1,0:T(4,128)} all-to-all(f32[16,4,128]{2,1,0:T(4,128)S(1)} %bitcast.41), channel_id=1, replica_groups=mesh['gen'=4,'dom'=4,'dp'=2] {'gen','dom'}, dimensions={0} | all-to-all | bytes 65536 | tf_op jit(solution)/shard_map/all_to_all | solution.py:316
  106.2 1.4 %shard_map.100 = (f32[1,128]{1,0:T(1,128)}, f32[1,8]{1,0:T(1,128)}) custom-call(s32[2]{0:T(128)} %copy-done.8, s32[4,128]{1,0:T(4,128)} %bitcast.31, f32[16,4,128]{2,1,0:T(4,128)} %all_to_all.5.all_ref), custom_call_target="tpu_custom_call" | custom-call | tf_op jit(solution)/shard_map/pallas_call | solution.py:261
  (15 shorter events, 0.1 us)
Async XLA Ops:
  0.6 77.3 %copy-start.7 = (s32[512]{0:T(512)S(1)}, s32[512]{0:T(512)}, u32[]{:S(2)}) copy-start(s32[512]{0:T(512)} %param.14) | copy-start | bytes 6148
  0.6 77.3 %copy-start.5 = (f32[4096]{0:T(1024)S(1)}, f32[4096]{0:T(1024)}, u32[]{:S(2)}) copy-start(f32[4096]{0:T(1024)} %param.12) | copy-start | bytes 49156
  1.7 9.2 %collective-permute-start = (bf16[128,512]{1,0:T(8,128)(2,1)S(1)}, bf16[128,512]{1,0:T(8,128)(2,1)S(1)}, u32[]{:S(2)}, u32[]{:S(2)}) collective-permute-start(bf16[128,512]{1,0:T(8,128)(2,1)S(1)} %get-tuple-element.11.refs_0_), channel_id=1, source_target_pairs={{6,0},{0,2},{2,4},{4,6},{7,1},{1,3},{3,5},{5,7},{14,8},{8,10},{10,... | collective-permute-start | bytes 393224 | tf_op jit(solution)/shard_map/ppermute | solution.py:33
  4.8 20.1 %collective-permute-start.12 = (bf16[128,1024]{1,0:T(8,128)(2,1)}, bf16[128,1024]{1,0:T(8,128)(2,1)S(1)}, u32[]{:S(2)}, u32[]{:S(2)}) collective-permute-start(bf16[128,1024]{1,0:T(8,128)(2,1)} %refs_0_.1), channel_id=1, source_target_pairs={{8,0},{0,8},{24,16},{16,24},{9,1},{1,9},{25,17},{17,25},{10,2},{2,... | collective-permute-start | bytes 786440 | tf_op jit(solution)/shard_map/ppermute | solution.py:33
  6.2 20.2 %collective-permute-start.13 = (bf16[128,1024]{1,0:T(8,128)(2,1)}, bf16[128,1024]{1,0:T(8,128)(2,1)S(1)}, u32[]{:S(2)}, u32[]{:S(2)}) collective-permute-start(bf16[128,1024]{1,0:T(8,128)(2,1)} %refs_0_.1), channel_id=1, source_target_pairs={{16,0},{24,8},{0,16},{8,24},{17,1},{25,9},{1,17},{9,25},{18,2},{26... | collective-permute-start | bytes 786440 | tf_op jit(solution)/shard_map/ppermute | solution.py:33
  7.8 18.7 %collective-permute-start.14 = (bf16[128,1024]{1,0:T(8,128)(2,1)}, bf16[128,1024]{1,0:T(8,128)(2,1)S(1)}, u32[]{:S(2)}, u32[]{:S(2)}) collective-permute-start(bf16[128,1024]{1,0:T(8,128)(2,1)} %refs_0_.1), channel_id=1, source_target_pairs={{24,0},{16,8},{8,16},{0,24},{25,1},{17,9},{9,17},{1,25},{26,2},{18... | collective-permute-start | bytes 786440 | tf_op jit(solution)/shard_map/ppermute | solution.py:33
  8.2 8.9 %collective-permute-start.1 = (bf16[128,512]{1,0:T(8,128)(2,1)S(1)}, bf16[128,512]{1,0:T(8,128)(2,1)S(1)}, u32[]{:S(2)}, u32[]{:S(2)}) collective-permute-start(bf16[128,512]{1,0:T(8,128)(2,1)S(1)} %get-tuple-element.11.refs_0_), channel_id=1, source_target_pairs={{4,0},{6,2},{0,4},{2,6},{5,1},{7,3},{1,5},{3,7},{12,8},{14,10},{8,... | collective-permute-start | bytes 393224 | tf_op jit(solution)/shard_map/ppermute | solution.py:33
  10.8 8.8 %collective-permute-start.2 = (bf16[128,512]{1,0:T(8,128)(2,1)S(1)}, bf16[128,512]{1,0:T(8,128)(2,1)S(1)}, u32[]{:S(2)}, u32[]{:S(2)}) collective-permute-start(bf16[128,512]{1,0:T(8,128)(2,1)S(1)} %get-tuple-element.11.refs_0_), channel_id=1, source_target_pairs={{2,0},{4,2},{6,4},{0,6},{3,1},{5,3},{7,5},{1,7},{10,8},{12,10},{14... | collective-permute-start | bytes 393224 | tf_op jit(solution)/shard_map/ppermute | solution.py:33
  12.3 80.6 %copy-start.8 = (s32[2]{0:T(128)}, s32[2]{0:T(128)S(1)}, u32[]{:S(2)}) copy-start(s32[2]{0:T(128)S(1)} %pad_add_fusion.index_ref) | copy-start | bytes 28
  17.2 14.4 %collective-permute-start.6 = (bf16[128,512]{1,0:T(8,128)(2,1)S(1)}, bf16[128,512]{1,0:T(8,128)(2,1)S(1)}, u32[]{:S(2)}, u32[]{:S(2)}) collective-permute-start(bf16[128,512]{1,0:T(8,128)(2,1)S(1)} %get-tuple-element.10.refs_0_), channel_id=1, source_target_pairs={{6,0},{0,2},{2,4},{4,6},{7,1},{1,3},{3,5},{5,7},{14,8},{8,10},{10,... | collective-permute-start | bytes 393224 | tf_op jit(solution)/shard_map/ppermute | solution.py:33
  19.7 12.0 %collective-permute-start.7 = (bf16[128,512]{1,0:T(8,128)(2,1)S(1)}, bf16[128,512]{1,0:T(8,128)(2,1)S(1)}, u32[]{:S(2)}, u32[]{:S(2)}) collective-permute-start(bf16[128,512]{1,0:T(8,128)(2,1)S(1)} %get-tuple-element.10.refs_0_), channel_id=1, source_target_pairs={{4,0},{6,2},{0,4},{2,6},{5,1},{7,3},{1,5},{3,7},{12,8},{14,10},{8,... | collective-permute-start | bytes 393224 | tf_op jit(solution)/shard_map/ppermute | solution.py:33
  23.0 0.7 copy-start
  24.8 19.8 %collective-permute-start.3 = (bf16[272,512]{1,0:T(8,128)(2,1)S(1)}, bf16[272,512]{1,0:T(8,128)(2,1)S(1)}, u32[]{:S(2)}, u32[]{:S(2)}) collective-permute-start(bf16[272,512]{1,0:T(8,128)(2,1)S(1)} %shard_map.95.refs_0_), channel_id=1, source_target_pairs={{8,0},{0,8},{24,16},{16,24},{9,1},{1,9},{25,17},{17,25},{10,2},{2,... | collective-permute-start | bytes 835592 | tf_op jit(solution)/shard_map/ppermute | solution.py:33
  26.5 7.8 %collective-permute-start.8 = (bf16[128,512]{1,0:T(8,128)(2,1)S(1)}, bf16[128,512]{1,0:T(8,128)(2,1)S(1)}, u32[]{:S(2)}, u32[]{:S(2)}) collective-permute-start(bf16[128,512]{1,0:T(8,128)(2,1)S(1)} %get-tuple-element.10.refs_0_), channel_id=1, source_target_pairs={{2,0},{4,2},{6,4},{0,6},{3,1},{5,3},{7,5},{1,7},{10,8},{12,10},{14... | collective-permute-start | bytes 393224 | tf_op jit(solution)/shard_map/ppermute | solution.py:33
  26.5 0.7 copy-start.1
  27.2 0.9 copy-start.9
  29.5 8.1 %collective-permute-start.15 = (bf16[272,256]{1,0:T(8,128)(2,1)S(1)}, bf16[272,256]{1,0:T(8,128)(2,1)S(1)}, u32[]{:S(2)}, u32[]{:S(2)}) collective-permute-start(bf16[272,256]{1,0:T(8,128)(2,1)S(1)} %get-tuple-element.7), channel_id=1, source_target_pairs={{6,0},{0,2},{2,4},{4,6},{7,1},{1,3},{3,5},{5,7},{14,8},{8,10},{10,... | collective-permute-start | bytes 417800 | tf_op jit(solution)/shard_map/ppermute | solution.py:33
  31.6 9.9 %collective-permute-start.16 = (bf16[272,256]{1,0:T(8,128)(2,1)S(1)}, bf16[272,256]{1,0:T(8,128)(2,1)S(1)}, u32[]{:S(2)}, u32[]{:S(2)}) collective-permute-start(bf16[272,256]{1,0:T(8,128)(2,1)S(1)} %get-tuple-element.7), channel_id=1, source_target_pairs={{4,0},{6,2},{0,4},{2,6},{5,1},{7,3},{1,5},{3,7},{12,8},{14,10},{8,... | collective-permute-start | bytes 417800 | tf_op jit(solution)/shard_map/ppermute | solution.py:33
  31.6 11.6 %collective-permute-start.17 = (bf16[272,256]{1,0:T(8,128)(2,1)S(1)}, bf16[272,256]{1,0:T(8,128)(2,1)S(1)}, u32[]{:S(2)}, u32[]{:S(2)}) collective-permute-start(bf16[272,256]{1,0:T(8,128)(2,1)S(1)} %get-tuple-element.7), channel_id=1, source_target_pairs={{2,0},{4,2},{6,4},{0,6},{3,1},{5,3},{7,5},{1,7},{10,8},{12,10},{14... | collective-permute-start | bytes 417800 | tf_op jit(solution)/shard_map/ppermute | solution.py:33
  34.2 10.9 %collective-permute-start.4 = (bf16[272,512]{1,0:T(8,128)(2,1)S(1)}, bf16[272,512]{1,0:T(8,128)(2,1)S(1)}, u32[]{:S(2)}, u32[]{:S(2)}) collective-permute-start(bf16[272,512]{1,0:T(8,128)(2,1)S(1)} %shard_map.95.refs_0_), channel_id=1, source_target_pairs={{16,0},{24,8},{0,16},{8,24},{17,1},{25,9},{1,17},{9,25},{18,2},{26... | collective-permute-start | bytes 835592 | tf_op jit(solution)/shard_map/ppermute | solution.py:33
  35.8 0.7 copy-start.2
  37.6 11.5 %collective-permute-start.5 = (bf16[272,512]{1,0:T(8,128)(2,1)S(1)}, bf16[272,512]{1,0:T(8,128)(2,1)S(1)}, u32[]{:S(2)}, u32[]{:S(2)}) collective-permute-start(bf16[272,512]{1,0:T(8,128)(2,1)S(1)} %shard_map.95.refs_0_), channel_id=1, source_target_pairs={{24,0},{16,8},{8,16},{0,24},{25,1},{17,9},{9,17},{1,25},{26,2},{18... | collective-permute-start | bytes 835592 | tf_op jit(solution)/shard_map/ppermute | solution.py:33
  41.5 13.5 %collective-permute-start.9 = (bf16[272,512]{1,0:T(8,128)(2,1)S(1)}, bf16[272,512]{1,0:T(8,128)(2,1)S(1)}, u32[]{:S(2)}, u32[]{:S(2)}) collective-permute-start(bf16[272,512]{1,0:T(8,128)(2,1)S(1)} %shard_map.96.refs_4_), channel_id=1, source_target_pairs={{8,0},{0,8},{24,16},{16,24},{9,1},{1,9},{25,17},{17,25},{10,2},{2,... | collective-permute-start | bytes 835592 | tf_op jit(solution)/shard_map/ppermute | solution.py:33
  43.2 15.5 %collective-permute-start.10 = (bf16[272,512]{1,0:T(8,128)(2,1)S(1)}, bf16[272,512]{1,0:T(8,128)(2,1)S(1)}, u32[]{:S(2)}, u32[]{:S(2)}) collective-permute-start(bf16[272,512]{1,0:T(8,128)(2,1)S(1)} %shard_map.96.refs_4_), channel_id=1, source_target_pairs={{16,0},{24,8},{0,16},{8,24},{17,1},{25,9},{1,17},{9,25},{18,2},{26... | collective-permute-start | bytes 835592 | tf_op jit(solution)/shard_map/ppermute | solution.py:33
  44.7 16.3 %collective-permute-start.11 = (bf16[272,512]{1,0:T(8,128)(2,1)S(1)}, bf16[272,512]{1,0:T(8,128)(2,1)S(1)}, u32[]{:S(2)}, u32[]{:S(2)}) collective-permute-start(bf16[272,512]{1,0:T(8,128)(2,1)S(1)} %shard_map.96.refs_4_), channel_id=1, source_target_pairs={{24,0},{16,8},{8,16},{0,24},{25,1},{17,9},{9,17},{1,25},{26,2},{18... | collective-permute-start | bytes 835592 | tf_op jit(solution)/shard_map/ppermute | solution.py:33
  45.1 32.8 %collective-permute-start.18 = (bf16[272,768]{1,0:T(8,128)(2,1)S(1)}, bf16[272,768]{1,0:T(8,128)(2,1)S(1)}, u32[]{:S(2)}, u32[]{:S(2)}) collective-permute-start(bf16[272,768]{1,0:T(8,128)(2,1)S(1)} %constant_dynamic-update-slice_fusion.refs_1_), channel_id=1, source_target_pairs={{8,0},{0,8},{24,16},{16,24},{9,1},{1,9},{25,17},{17,25},{10,2},{2,... | collective-permute-start | bytes 1253384 | tf_op jit(solution)/shard_map/ppermute | solution.py:33
  49.1 28.8 %collective-permute-start.19 = (bf16[272,768]{1,0:T(8,128)(2,1)S(1)}, bf16[272,768]{1,0:T(8,128)(2,1)S(1)}, u32[]{:S(2)}, u32[]{:S(2)}) collective-permute-start(bf16[272,768]{1,0:T(8,128)(2,1)S(1)} %constant_dynamic-update-slice_fusion.refs_1_), channel_id=1, source_target_pairs={{16,0},{24,8},{0,16},{8,24},{17,1},{25,9},{1,17},{9,25},{18,2},{26... | collective-permute-start | bytes 1253384 | tf_op jit(solution)/shard_map/ppermute | solution.py:33
  55.1 22.8 %collective-permute-start.20 = (bf16[272,768]{1,0:T(8,128)(2,1)S(1)}, bf16[272,768]{1,0:T(8,128)(2,1)S(1)}, u32[]{:S(2)}, u32[]{:S(2)}) collective-permute-start(bf16[272,768]{1,0:T(8,128)(2,1)S(1)} %constant_dynamic-update-slice_fusion.refs_1_), channel_id=1, source_target_pairs={{24,0},{16,8},{8,16},{0,24},{25,1},{17,9},{9,17},{1,25},{26,2},{18... | collective-permute-start | bytes 1253384 | tf_op jit(solution)/shard_map/ppermute | solution.py:33
  61.0 0.7 copy-start.3
  61.7 0.7 copy-start.4
  62.4 0.7 copy-start.6
where the time goes:
time: 108 us
  starting transfers between devices  37.5 us (35%)
  Pallas kernels  34.7 us (32%)
  waiting for transfers between devices  14.7 us (14%)
  blocking collectives  13.4 us (12%)
  local copies, waits for them, and re-layouts  6.29 us (6%)
    ppermute x21, starting transfers between devices, around(): parts.append(lax.ppermute(block, axis, pairs))  37.5 us
    pallas_call x2, Pallas kernels, stats(): pl.pallas_call(functools.partial(stats_kernel, tuple(pieces), buffers), g...  29.7 us
    ppermute x21, waiting for transfers between devices, around(): parts.append(lax.ppermute(block, axis, pairs))  14.7 us
    all_to_all x1, blocking collectives, per_device(): gathered = lax.all_to_all(sent, ('gen', 'dom'), 0, 0)  13.4 us
    unnamed x22, local copies, waits for them, and re-layouts  5.1 us
    pallas_call x3, Pallas kernels, compact(): pl.pallas_call(functools.partial(compact_kernel, pack_axis, spans), out_s...  3.61 us
  transfers between devices with their start and end apart: 21, of which 5 were waited for; matrix products, arithmetic and copies ran while one was open for 0% of the time, Pallas kernels for 17%

commit v1 on v0

v1 whole, which is shorter than its diff:
```python
import functools

import jax
import jax.numpy as jnp
from jax import lax
from jax.experimental import pallas as pl
from jax.experimental.pallas import tpu as pltpu
from jax.sharding import PartitionSpec as P


DOC_PACK = 8
EPS = 1e-05
PORTIONS = (3, 5)
VMEM = pltpu.VMEM


def whole(memory_space=VMEM):
    return pl.BlockSpec(memory_space=memory_space)


def origin(axis, index, k, count):
    if axis == "gen" and count & (count - 1) == 0:
        return index ^ k
    return (index - k + count) % count


def portions(width):
    edges, done = [0], 0
    for portion in PORTIONS[:-1]:
        done += portion
        edge = max(width * done // sum(PORTIONS) // 128 * 128, edges[-1] + 128)
        edges.append(edge)
    edges.append(width)
    return list(zip(edges, edges[1:]))


def around(block, axis):
    count = lax.axis_size(axis)
    parts = [block]
    for k in range(1, count):
        pairs = [(origin(axis, i, k, count), i) for i in range(count)]
        parts.append(lax.ppermute(block, axis, pairs))
    return parts


def pack_extents(doc):
    live = jnp.where(doc >= 0, 1.0, 0.0)
    counts = jnp.sum(live, axis=1, keepdims=True)
    ahead = jnp.zeros((1, 1), jnp.float32)
    extents = []
    for p in range(doc.shape[0]):
        count = counts[p : p + 1, :]
        extents.append((count, ahead))
        ahead = ahead + count
    return extents


def slot_mask(extent, slots, rows):
    count, ahead = extent
    slot = lax.broadcasted_iota(jnp.int32, (slots, rows), 0).astype(jnp.float32)
    row = lax.broadcasted_iota(jnp.int32, (slots, rows), 1).astype(jnp.float32)
    return (slot - ahead == row) & (row < count)


def prepare_kernel(vocab, *refs):
    doc_ref, target_ref, gen_gain_ref, dom_gain_ref, rows_ref = refs[:5]
    doc_out, live_ref, wanted_ref, gen_gain_out, dom_gain_out, rows_out = refs[5:]
    doc_out[...] = doc_ref[...]
    gen_gain_out[...] = gen_gain_ref[...]
    dom_gain_out[...] = dom_gain_ref[...]
    rows_out[...] = rows_ref[...]
    packs, rows = doc_ref.shape
    slots = live_ref.shape[0]
    extents = pack_extents(doc_ref[...])
    device = lax.axis_index("gen") * lax.axis_size("dom") + lax.axis_index("dom")
    ids = jnp.zeros((slots, 1), jnp.float32)
    for p in range(packs):
        mask = slot_mask(extents[p], slots, rows)
        live_ref[:, p * rows : (p + 1) * rows] = jnp.where(mask, 1.0, 0.0).astype(jnp.bfloat16)
        row = (target_ref[p : p + 1, :] - device * vocab).astype(jnp.float32)
        ids = ids + jnp.sum(jnp.where(mask, row, 0.0), axis=1, keepdims=True)
    wanted_ref[...] = jnp.broadcast_to(ids.astype(jnp.int32), wanted_ref.shape)


def prepare(doc, target, gen_gain, dom_gain, rows_in, slots, vocab):
    like = lambda x: jax.ShapeDtypeStruct(x.shape, x.dtype)
    return pl.pallas_call(
        functools.partial(prepare_kernel, vocab),
        out_shape=(
            like(doc),
            jax.ShapeDtypeStruct((slots, doc.size), jnp.bfloat16),
            jax.ShapeDtypeStruct((slots, 128), jnp.int32),
            like(gen_gain),
            like(dom_gain),
            like(rows_in),
        ),
        in_specs=[whole()] * 5,
        out_specs=[whole()] * 6,
        compiler_params=pltpu.CompilerParams(vmem_limit_bytes=8 * 1024 * 1024),
    )(doc, target, gen_gain, dom_gain, rows_in)


def compact_kernel(pack_axis, spans, live_ref, *refs):
    part_refs = refs[:-2] if spans else refs[:-1]
    out_ref = refs[len(part_refs)]
    rows = part_refs[0].shape[0]
    mine = lax.axis_index(pack_axis)
    total = None
    for k, part_ref in enumerate(part_refs):
        pack = origin(pack_axis, mine, k, len(part_refs))
        live = live_ref[:, pl.ds(pl.multiple_of(pack * rows, rows), rows)]
        piece = jnp.dot(live, part_ref[...], preferred_element_type=jnp.float32)
        total = piece if total is None else total + piece
    out_ref[...] = total.astype(jnp.bfloat16)
    if spans:
        span_ref = refs[-1]
        width = span_ref.shape[1]
        start = pl.multiple_of(mine * width, width)
        span_ref[...] = out_ref[:, pl.ds(start, width)]


def compact(parts, live, pack_axis, spans=0):
    width = parts[0].shape[1]
    slots = live.shape[0]
    out_shape = [jax.ShapeDtypeStruct((slots, width), jnp.bfloat16)]
    if spans:
        out_shape.append(jax.ShapeDtypeStruct((slots, width // spans), jnp.bfloat16))
    return pl.pallas_call(
        functools.partial(compact_kernel, pack_axis, spans),
        out_shape=out_shape,
        in_specs=[whole()] * (1 + len(parts)),
        out_specs=[whole()] * len(out_shape),
        compiler_params=pltpu.CompilerParams(vmem_limit_bytes=16 * 1024 * 1024),
        cost_estimate=pl.CostEstimate(
            flops=2 * width * live.size,
            bytes_accessed=2 * width * (live.shape[1] + slots),
            transcendentals=0,
        ),
    )(live, *parts)


def tally(logits, wanted, top, total, picked):
    lanes = top.shape[1]
    groups = [logits[:, at : at + lanes] for at in range(0, logits.shape[1], lanes)]
    former = top[...]
    highest = functools.reduce(jnp.maximum, groups, former)
    lane = lax.broadcasted_iota(jnp.int32, former.shape, 1)
    away = wanted - lane
    latest = total[...] * jnp.exp(former - highest)
    hit = picked[...]
    for k, group in enumerate(groups):
        latest = latest + jnp.exp(group - highest)
        hit = jnp.where(away == k * lanes, group, hit)
    top[...] = highest
    total[...] = latest
    picked[...] = hit


def summed_up(top, total, picked):
    highest = jnp.max(top[...], axis=1, keepdims=True)
    everything = jnp.sum(total[...] * jnp.exp(top[...] - highest), axis=1, keepdims=True)
    return highest + jnp.log(everything), jnp.sum(picked[...], axis=1, keepdims=True)


def stats_kernel(pieces, buffers, wanted_ref, live_ref, gain_ref, head_ref, *refs):
    part_count = pieces[-1][0] + 1
    part_refs = refs[:part_count]
    out_ref, normed, tiles, sems, top, total, picked = refs[part_count:]
    slots, width = normed.shape
    tile = tiles.shape[1]
    packs, _, rows = out_ref.shape
    j = pl.program_id(0)
    steps = pl.num_programs(0)

    def copy(step):
        slot = lax.rem(step, buffers)
        return pltpu.make_async_copy(
            head_ref.at[pl.ds(pl.multiple_of(step * tile, tile), tile), :],
            tiles.at[slot],
            sems.at[slot],
        )

    @pl.when(j == 0)
    def _():
        copy(0).start()
        for step in range(1, buffers - 1):
            pl.when(step < steps)(lambda: copy(step).start())

    @pl.when(j + buffers - 1 < steps)
    def _():
        copy(j + buffers - 1).start()

    @pl.when(j == 0)
    def _():
        sums = jnp.zeros((slots, 1), jnp.float32)
        for part_ref in part_refs:
            values = part_ref[...].astype(jnp.float32)
            sums = sums + jnp.sum(values * values, axis=1, keepdims=True)
        scale = lax.rsqrt(sums / width + EPS)
        for part, start, extent, place in pieces:
            at = pl.ds(pl.multiple_of(place(), 128), extent)
            values = part_refs[part][:, start : start + extent].astype(jnp.float32)
            normed[:, at] = (values * scale * gain_ref[:, at]).astype(jnp.bfloat16)
        top[...] = jnp.full(top.shape, -jnp.inf, jnp.float32)
        total[...] = jnp.zeros(total.shape, jnp.float32)
        picked[...] = jnp.zeros(picked.shape, jnp.float32)

    copy(j).wait()
    logits = lax.dot_general(
        normed[...],
        tiles[lax.rem(j, buffers)],
        (((1,), (1,)), ((), ())),
        preferred_element_type=jnp.float32,
    )
    tally(logits, wanted_ref[...] - j * tile, top, total, picked)

    @pl.when(j == steps - 1)
    def _():
        log_total, logit = summed_up(top, total, picked)
        for p in range(packs):
            mask = live_ref[:, p * rows : (p + 1) * rows].astype(jnp.float32) > 0.5
            out_ref[p, 0:1, :] = jnp.sum(jnp.where(mask, log_total, 0.0), axis=0, keepdims=True)
            out_ref[p, 1:2, :] = jnp.sum(jnp.where(mask, logit, 0.0), axis=0, keepdims=True)


def stats(parts, gain, head, wanted, live, packs):
    slots = parts[0][0].shape[0]
    vocab, width = head.shape
    rows = live.shape[1] // packs
    tile = min(512, vocab)
    buffers = 3
    pieces = []
    for number, (array, places) in enumerate(parts):
        extent = array.shape[1] // len(places)
        for k, place in enumerate(places):
            pieces.append((number, k * extent, extent, place))
    column = VMEM((slots, 128), jnp.float32)
    return pl.pallas_call(
        functools.partial(stats_kernel, tuple(pieces), buffers),
        grid=(vocab // tile,),
        in_specs=[whole(), whole(), whole(), whole(pl.ANY)] + [whole() for _ in parts],
        out_specs=whole(),
        out_shape=jax.ShapeDtypeStruct((packs, 2, rows), jnp.float32),
        scratch_shapes=[
            VMEM((slots, width), jnp.bfloat16),
            VMEM((buffers, tile, width), jnp.bfloat16),
            pltpu.SemaphoreType.DMA((buffers,)),
            column,
            column,
            column,
        ],
        compiler_params=pltpu.CompilerParams(vmem_limit_bytes=32 * 1024 * 1024),
        cost_estimate=pl.CostEstimate(
            flops=2 * slots * width * vocab,
            bytes_accessed=2 * width * (vocab + slots),
            transcendentals=slots * vocab,
        ),
    )(wanted, live, gain, head, *[array for array, _ in parts])


def finish_kernel(doc_ref, all_ref, token_ref, score_ref):
    pack = lax.axis_index("dom")
    members = all_ref.shape[0]
    both = all_ref[...]

    def log_prob(at):
        logs = [both[i, at : at + 1, :] for i in range(members)]
        highest = functools.reduce(jnp.maximum, logs)
        summed = functools.reduce(jnp.add, [jnp.exp(one - highest) for one in logs])
        logit = functools.reduce(jnp.add, [both[i, at + 1 : at + 2, :] for i in range(members)])
        return logit - (highest + jnp.log(summed))

    ids = doc_ref[pl.ds(pack, 1), :]
    diff = jnp.where(ids >= 0, log_prob(2) - log_prob(0), 0.0)
    token_ref[...] = diff
    rows = ids.shape[1]
    number = lax.broadcasted_iota(jnp.int32, (DOC_PACK, rows), 0) + pack * DOC_PACK
    mine = number == ids
    sums = jnp.sum(jnp.where(mine, diff, 0.0), axis=1, keepdims=True)
    counts = jnp.sum(jnp.where(mine, 1.0, 0.0), axis=1, keepdims=True)
    score = sums / counts
    row = lax.broadcasted_iota(jnp.int32, (DOC_PACK, DOC_PACK), 0)
    column = lax.broadcasted_iota(jnp.int32, (DOC_PACK, DOC_PACK), 1)
    score_ref[...] = jnp.sum(jnp.where(row == column, score, 0.0), axis=0, keepdims=True)


def finish(gathered, doc):
    rows = doc.shape[1]
    token, score = pl.pallas_call(
        finish_kernel,
        out_shape=(
            jax.ShapeDtypeStruct((1, rows), jnp.float32),
            jax.ShapeDtypeStruct((1, DOC_PACK), jnp.float32),
        ),
        in_specs=[whole(), whole()],
        out_specs=(whole(), whole()),
        compiler_params=pltpu.CompilerParams(vmem_limit_bytes=8 * 1024 * 1024),
    )(doc, gathered)
    return token.reshape(rows), score.reshape(DOC_PACK)


def per_device(gen_hidden, gen_gain, gen_head, dom_hidden, dom_gain, dom_head, targets, doc_ids):
    rows = gen_hidden.shape[0]
    gen_count = lax.axis_size("gen")
    dom_count = lax.axis_size("dom")
    doc = doc_ids.reshape(dom_count, rows)
    target = targets.reshape(dom_count, rows)
    slots = dom_count // 2 * (rows + DOC_PACK)
    width = gen_head.shape[1]
    block_width = gen_hidden.shape[1]
    cuts = portions(block_width)
    dom_width = dom_hidden.shape[1]
    spans = gen_count if dom_width % (gen_count * 128) == 0 else 0
    gen_from = lambda k: origin("gen", lax.axis_index("gen"), k, gen_count)
    dom_from = lambda k: origin("dom", lax.axis_index("dom"), k, dom_count)
    doc, live, wanted, gen_gain, dom_gain, dom_own = prepare(
        doc, target, gen_gain.reshape(1, width), dom_gain.reshape(1, width), dom_hidden,
        slots, gen_head.shape[0],
    )
    gen_first = [around(gen_hidden[:, start:stop], "dom") for start, stop in cuts]
    dom_first = around(dom_hidden, "gen")
    gen_parts = []
    for h, (start, _) in enumerate(cuts):
        (rows_in,) = compact(gen_first[h], live, "dom")
        for k, part in enumerate(around(rows_in, "gen")):
            place = lambda k=k, start=start: gen_from(k) * block_width + start
            gen_parts.append((part, [place]))
    dom_rows, *dom_span = compact([dom_own] + dom_first[1:], live, "gen", spans)
    dom_parts = [(dom_rows, [lambda: dom_from(0) * dom_width])]
    if spans:
        span = dom_width // spans
        received = around(dom_span[0], "dom")[1:]
        joined = jnp.concatenate(received, axis=1)
        for k, part in enumerate(around(joined, "gen")):
            places = [
                lambda k=k, i=i: dom_from(i) * dom_width + gen_from(k) * span
                for i in range(1, dom_count)
            ]
            dom_parts.append((part, places))
    else:
        for k, part in enumerate(around(dom_rows, "dom")[1:]):
            dom_parts.append((part, [lambda k=k: dom_from(k + 1) * dom_width]))
    gen_stats = stats(gen_parts, gen_gain, gen_head, wanted, live, dom_count)
    dom_stats = stats(dom_parts, dom_gain, dom_head, wanted, live, dom_count)
    both = jnp.concatenate([gen_stats, dom_stats], axis=1)
    sent = jnp.broadcast_to(both[None], (gen_count,) + both.shape)
    sent = sent.reshape((gen_count * dom_count,) + both.shape[1:])
    gathered = lax.all_to_all(sent, ("gen", "dom"), 0, 0)
    return finish(gathered, doc)


def solution(mesh):
    in_specs = (
        P(("dp", "dom"), "gen"),
        P("dp"),
        P(("dp", "gen", "dom"), None),
        P(("dp", "gen"), "dom"),
        P("dp"),
        P(("dp", "gen", "dom"), None),
        P("dp"),
        P("dp"),
    )
    out_specs = (P(("dp", "dom")), P(("dp", "dom")))
    return jax.shard_map(
        per_device, mesh=mesh, in_specs=in_specs, out_specs=out_specs, check_vma=False
    )
```

time: 108 us -> 118 us (1.093)
  waiting for transfers between devices: 14.7 us -> 29.5 us
  Pallas kernels: 34.7 us -> 31.2 us
  blocking collectives: 13.4 us -> 10.5 us
  starting transfers between devices: 37.5 us -> 39.5 us
    ppermute x21, waiting for transfers between devices: 14.7 us -> 29.5 us  [around(): parts.append(lax.ppermute(block, axis, pairs))]
    all_to_all x1, blocking collectives: 13.4 us -> 10.5 us  [per_device(): gathered = lax.all_to_all(sent, ('gen', 'dom'), 0, 0)]
    ppermute x21, starting transfers between devices: 37.5 us -> 39.5 us  [around(): parts.append(lax.ppermute(block, axis, pairs))]
    pallas_call x3, Pallas kernels: 3.61 us -> 1.76 us  [compact(): pl.pallas_call(functools.partial(compact_kernel, pack_axis, spans), out_s...]
    unnamed x22 -> x12, local copies, waits for them, and re-layouts: 5.1 us -> 3.77 us
    pallas_call x2, Pallas kernels: 29.7 us -> 28.5 us  [stats(): pl.pallas_call(functools.partial(stats_kernel, tuple(pieces), buffers), g...]
  transfers between devices with their start and end apart: 21 -> 21, of which waited for: 5 -> 4; matrix products, arithmetic and copies ran while one was open for 0% -> 2% of each run, Pallas kernels for 17% -> 14%
where the time goes in v1:
time: 118 us; the launch traced here: 117 us
  starting transfers between devices  39.5 us (33%)
  Pallas kernels  31.2 us (26%)
  waiting for transfers between devices  29.5 us (25%)
  blocking collectives  10.5 us (9%)
  local copies, waits for them, and re-layouts  5.62 us (5%)
    ppermute x21, starting transfers between devices, around(): parts.append(lax.ppermute(block, axis, pairs))  39.5 us
    ppermute x21, waiting for transfers between devices, around(): parts.append(lax.ppermute(block, axis, pairs))  29.5 us
    pallas_call x2, Pallas kernels, stats(): pl.pallas_call(functools.partial(stats_kernel, tuple(pieces), buffers), g...  28.5 us
    all_to_all x1, blocking collectives, per_device(): gathered = lax.all_to_all(sent, ('gen', 'dom'), 0, 0)  10.5 us
    unnamed x12, local copies, waits for them, and re-layouts  3.77 us
  transfers between devices with their start and end apart: 21, of which 4 were waited for; matrix products, arithmetic and copies ran while one was open for 2% of the time, Pallas kernels for 14%

profile of v1, /device:TPU:0, one launch (start us, length us, event | category | flops | bytes accessed | tf_op | source)
XLA Modules:
  0.0 117.2 jit_solution(12811902316287499083)
XLA Ops:
  0.6 3.0 %collective-permute-start.12 = (bf16[128,1024]{1,0:T(8,128)(2,1)}, bf16[128,1024]{1,0:T(8,128)(2,1)S(1)}, u32[]{:S(2)}, u32[]{:S(2)}) collective-permute-start(bf16[128,1024]{1,0:T(8,128)(2,1)} %refs_4_.1), channel_id=1, source_target_pairs={{8,0},{0,8},{24,16},{16,24},{9,1},{1,9},{25,17},{17,25},{10,2},{2,... | collective-permute-start | bytes 786440 | tf_op jit(solution)/shard_map/ppermute | solution.py:42
  3.7 1.5 %collective-permute-start.13 = (bf16[128,1024]{1,0:T(8,128)(2,1)}, bf16[128,1024]{1,0:T(8,128)(2,1)S(1)}, u32[]{:S(2)}, u32[]{:S(2)}) collective-permute-start(bf16[128,1024]{1,0:T(8,128)(2,1)} %refs_4_.1), channel_id=1, source_target_pairs={{16,0},{24,8},{0,16},{8,24},{17,1},{25,9},{1,17},{9,25},{18,2},{26... | collective-permute-start | bytes 786440 | tf_op jit(solution)/shard_map/ppermute | solution.py:42
  5.2 0.0 collective-permute-start.14
  5.2 0.9 slice.6.refs_0_
  6.1 2.1 %collective-permute-start = (bf16[128,384]{1,0:T(8,128)(2,1)S(1)}, bf16[128,384]{1,0:T(8,128)(2,1)S(1)}, u32[]{:S(2)}, u32[]{:S(2)}) collective-permute-start(bf16[128,384]{1,0:T(8,128)(2,1)S(1)} %slice.6.refs_0_), channel_id=1, source_target_pairs={{6,0},{0,2},{2,4},{4,6},{7,1},{1,3},{3,5},{5,7},{14,8},{8,10},{10,... | collective-permute-start | bytes 294920 | tf_op jit(solution)/shard_map/ppermute | solution.py:42
  8.2 2.6 %collective-permute-start.1 = (bf16[128,384]{1,0:T(8,128)(2,1)S(1)}, bf16[128,384]{1,0:T(8,128)(2,1)S(1)}, u32[]{:S(2)}, u32[]{:S(2)}) collective-permute-start(bf16[128,384]{1,0:T(8,128)(2,1)S(1)} %slice.6.refs_0_), channel_id=1, source_target_pairs={{4,0},{6,2},{0,4},{2,6},{5,1},{7,3},{1,5},{3,7},{12,8},{14,10},{8,... | collective-permute-start | bytes 294920 | tf_op jit(solution)/shard_map/ppermute | solution.py:42
  10.8 2.7 %collective-permute-done.refs_1_ = bf16[128,384]{1,0:T(8,128)(2,1)S(1)} collective-permute-done((bf16[128,384]{1,0:T(8,128)(2,1)S(1)}, bf16[128,384]{1,0:T(8,128)(2,1)S(1)}, u32[]{:S(2)}, u32[]{:S(2)}) %collective-permute-start) | collective-permute-done | bytes 98336 | tf_op jit(solution)/shard_map/ppermute | solution.py:42
  13.5 1.4 %collective-permute-start.2 = (bf16[128,384]{1,0:T(8,128)(2,1)S(1)}, bf16[128,384]{1,0:T(8,128)(2,1)S(1)}, u32[]{:S(2)}, u32[]{:S(2)}) collective-permute-start(bf16[128,384]{1,0:T(8,128)(2,1)S(1)} %slice.6.refs_0_), channel_id=1, source_target_pairs={{2,0},{4,2},{6,4},{0,6},{3,1},{5,3},{7,5},{1,7},{10,8},{12,10},{14... | collective-permute-start | bytes 294920 | tf_op jit(solution)/shard_map/ppermute | solution.py:42
  15.0 0.0 copy-start
  15.0 0.9 copy-done
  15.9 0.0 copy-start.1
  15.9 0.7 copy-done.1
  16.6 0.0 copy-start.2
  16.6 0.7 copy-done.2
  17.4 0.0 copy-start.3
  17.4 0.7 copy-done.3
  18.0 0.0 copy-start.4
  18.0 0.7 copy-done.4
  18.7 0.3 shard_map.95
  19.1 0.0 collective-permute-done.1.refs_2_
  19.1 0.0 collective-permute-done.2.refs_3_
  19.1 0.4 shard_map.96.refs_0_
  19.5 1.6 %collective-permute-start.3 = (bf16[272,384]{1,0:T(8,128)(2,1)S(1)}, bf16[272,384]{1,0:T(8,128)(2,1)S(1)}, u32[]{:S(2)}, u32[]{:S(2)}) collective-permute-start(bf16[272,384]{1,0:T(8,128)(2,1)S(1)} %shard_map.96.refs_0_), channel_id=1, source_target_pairs={{8,0},{0,8},{24,16},{16,24},{9,1},{1,9},{25,17},{17,25},{10,2},{2,... | collective-permute-start | bytes 626696 | tf_op jit(solution)/shard_map/ppermute | solution.py:42
  21.1 0.9 slice.7.refs_0_
  22.0 0.6 collective-permute-start.6
  22.6 0.0 collective-permute-done.12.refs_1_
  22.6 2.3 %collective-permute-start.7 = (bf16[128,640]{1,0:T(8,128)(2,1)S(1)}, bf16[128,640]{1,0:T(8,128)(2,1)S(1)}, u32[]{:S(2)}, u32[]{:S(2)}) collective-permute-start(bf16[128,640]{1,0:T(8,128)(2,1)S(1)} %slice.7.refs_0_), channel_id=1, source_target_pairs={{4,0},{6,2},{0,4},{2,6},{5,1},{7,3},{1,5},{3,7},{12,8},{14,10},{8,... | collective-permute-start | bytes 491528 | tf_op jit(solution)/shard_map/ppermute | solution.py:42
  24.9 0.0 collective-permute-done.13.refs_2_
  24.9 1.0 collective-permute-start.8
  26.0 0.0 collective-permute-done.14.refs_3_
  26.0 0.8 shard_map.99
  26.7 1.1 collective-permute-start.15
  27.8 3.2 %collective-permute-done.6.refs_1_ = bf16[128,640]{1,0:T(8,128)(2,1)S(1)} collective-permute-done((bf16[128,640]{1,0:T(8,128)(2,1)S(1)}, bf16[128,640]{1,0:T(8,128)(2,1)S(1)}, u32[]{:S(2)}, u32[]{:S(2)}) %collective-permute-start.6) | collective-permute-done | bytes 163872 | tf_op jit(solution)/shard_map/ppermute | solution.py:42
  31.0 4.8 %collective-permute-start.16 = (bf16[272,256]{1,0:T(8,128)(2,1)S(1)}, bf16[272,256]{1,0:T(8,128)(2,1)S(1)}, u32[]{:S(2)}, u32[]{:S(2)}) collective-permute-start(bf16[272,256]{1,0:T(8,128)(2,1)S(1)} %get-tuple-element.19), channel_id=1, source_target_pairs={{4,0},{6,2},{0,4},{2,6},{5,1},{7,3},{1,5},{3,7},{12,8},{14,10},{8,... | collective-permute-start | bytes 417800 | tf_op jit(solution)/shard_map/ppermute | solution.py:42
  35.8 1.7 %collective-permute-done.7.refs_2_ = bf16[128,640]{1,0:T(8,128)(2,1)S(1)} collective-permute-done((bf16[128,640]{1,0:T(8,128)(2,1)S(1)}, bf16[128,640]{1,0:T(8,128)(2,1)S(1)}, u32[]{:S(2)}, u32[]{:S(2)}) %collective-permute-start.7) | collective-permute-done | bytes 163872 | tf_op jit(solution)/shard_map/ppermute | solution.py:42
  37.6 8.0 %collective-permute-start.17 = (bf16[272,256]{1,0:T(8,128)(2,1)S(1)}, bf16[272,256]{1,0:T(8,128)(2,1)S(1)}, u32[]{:S(2)}, u32[]{:S(2)}) collective-permute-start(bf16[272,256]{1,0:T(8,128)(2,1)S(1)} %get-tuple-element.19), channel_id=1, source_target_pairs={{2,0},{4,2},{6,4},{0,6},{3,1},{5,3},{7,5},{1,7},{10,8},{12,10},{14... | collective-permute-start | bytes 417800 | tf_op jit(solution)/shard_map/ppermute | solution.py:42
  45.6 0.0 collective-permute-done.8.refs_3_
  45.6 0.6 shard_map.97.refs_4_
  46.2 0.6 collective-permute-start.9
  46.8 0.0 collective-permute-done.3.refs_1_
  46.8 1.5 %collective-permute-start.10 = (bf16[272,640]{1,0:T(8,128)(2,1)S(1)}, bf16[272,640]{1,0:T(8,128)(2,1)S(1)}, u32[]{:S(2)}, u32[]{:S(2)}) collective-permute-start(bf16[272,640]{1,0:T(8,128)(2,1)S(1)} %shard_map.97.refs_4_), channel_id=1, source_target_pairs={{16,0},{24,8},{0,16},{8,24},{17,1},{25,9},{1,17},{9,25},{18,2},{26... | collective-permute-start | bytes 1044488 | tf_op jit(solution)/shard_map/ppermute | solution.py:42
  48.3 0.0 collective-permute-done.15
  48.3 1.4 %collective-permute-start.11 = (bf16[272,640]{1,0:T(8,128)(2,1)S(1)}, bf16[272,640]{1,0:T(8,128)(2,1)S(1)}, u32[]{:S(2)}, u32[]{:S(2)}) collective-permute-start(bf16[272,640]{1,0:T(8,128)(2,1)S(1)} %shard_map.97.refs_4_), channel_id=1, source_target_pairs={{24,0},{16,8},{8,16},{0,24},{25,1},{17,9},{9,17},{1,25},{26,2},{18... | collective-permute-start | bytes 1044488 | tf_op jit(solution)/shard_map/ppermute | solution.py:42
  49.8 0.0 collective-permute-done.16
  49.8 1.6 %collective-permute-start.4 = (bf16[272,384]{1,0:T(8,128)(2,1)S(1)}, bf16[272,384]{1,0:T(8,128)(2,1)S(1)}, u32[]{:S(2)}, u32[]{:S(2)}) collective-permute-start(bf16[272,384]{1,0:T(8,128)(2,1)S(1)} %shard_map.96.refs_0_), channel_id=1, source_target_pairs={{16,0},{24,8},{0,16},{8,24},{17,1},{25,9},{1,17},{9,25},{18,2},{26... | collective-permute-start | bytes 626696 | tf_op jit(solution)/shard_map/ppermute | solution.py:42
  51.4 0.0 collective-permute-done.17
  51.4 0.5 collective-permute-start.5
  51.9 21.8 %collective-permute-done.4.refs_2_ = bf16[272,384]{1,0:T(8,128)(2,1)S(1)} collective-permute-done((bf16[272,384]{1,0:T(8,128)(2,1)S(1)}, bf16[272,384]{1,0:T(8,128)(2,1)S(1)}, u32[]{:S(2)}, u32[]{:S(2)}) %collective-permute-start.4) | collective-permute-done | bytes 208928 | tf_op jit(solution)/shard_map/ppermute | solution.py:42
  73.7 0.4 collective-permute-start.18
  74.1 0.0 collective-permute-done.5.refs_3_
  74.1 1.8 %collective-permute-start.19 = (bf16[272,768]{1,0:T(8,128)(2,1)S(1)}, bf16[272,768]{1,0:T(8,128)(2,1)S(1)}, u32[]{:S(2)}, u32[]{:S(2)}) collective-permute-start(bf16[272,768]{1,0:T(8,128)(2,1)S(1)} %constant_dynamic-update-slice_fusion.refs_1_), channel_id=1, source_target_pairs={{16,0},{24,8},{0,16},{8,24},{17,1},{25,9},{1,17},{9,25},{18,2},{26... | collective-permute-start | bytes 1253384 | tf_op jit(solution)/shard_map/ppermute | solution.py:42
  75.9 0.0 collective-permute-done.9.refs_5_
  75.9 1.5 %collective-permute-start.20 = (bf16[272,768]{1,0:T(8,128)(2,1)S(1)}, bf16[272,768]{1,0:T(8,128)(2,1)S(1)}, u32[]{:S(2)}, u32[]{:S(2)}) collective-permute-start(bf16[272,768]{1,0:T(8,128)(2,1)S(1)} %constant_dynamic-update-slice_fusion.refs_1_), channel_id=1, source_target_pairs={{24,0},{16,8},{8,16},{0,24},{25,1},{17,9},{9,17},{1,25},{26,2},{18... | collective-permute-start | bytes 1253384 | tf_op jit(solution)/shard_map/ppermute | solution.py:42
  77.4 0.0 collective-permute-done.10.refs_6_
  77.4 0.0 collective-permute-done.11.refs_7_
  77.4 14.2 %shard_map.98 = f32[4,2,128]{2,1,0:T(2,128)S(1)} custom-call(s32[272,128]{1,0:T(8,128)S(1)} %get-tuple-element.13.wanted_ref, bf16[272,512]{1,0:T(8,128)(2,1)S(1)} %get-tuple-element.14.live_ref, f32[1,4096]{1,0:T(1,128)S(1)} %get-tuple-element.15.gain_ref, bf16[4096,4096]{1,0:T(8,128)(2,1)} %head_ref.2, bf16[272,384]{1,0:T(8,128)(2,1)S(1)} %shard_map.96.refs_0_, ...), custom_call_target="tpu_custom_call" | custom-call | flops 9126805504 | bytes 35782656 | tf_op jit(solution)/shard_map/pallas_call | solution.py:238
  91.7 0.0 collective-permute-done.18.refs_2_
  91.7 0.0 collective-permute-done.19.refs_3_
  91.7 0.0 collective-permute-done.20.refs_4_
  91.7 14.2 %shard_map.100 = f32[4,2,128]{2,1,0:T(2,128)S(1)} custom-call(s32[272,128]{1,0:T(8,128)S(1)} %get-tuple-element.13.wanted_ref, bf16[272,512]{1,0:T(8,128)(2,1)S(1)} %get-tuple-element.14.live_ref, f32[1,4096]{1,0:T(1,128)S(1)} %get-tuple-element.16.gain_ref, bf16[4096,4096]{1,0:T(8,128)(2,1)} %head_ref.3, bf16[272,1024]{1,0:T(8,128)(2,1)S(1)} %get-tuple-element.18.refs_0_, ...), custom_call_target="tpu_custom_call" | custom-call | flops 9126805504 | bytes 35782656 | tf_op jit(solution)/shard_map/pallas_call | solution.py:238
  106.0 10.5 %all_to_all.5.all_ref = f32[16,4,128]{2,1,0:T(4,128)S(1)} all-to-all(f32[16,4,128]{2,1,0:T(4,128)S(1)} %bitcast.11), channel_id=1, replica_groups=mesh['gen'=4,'dom'=4,'dp'=2] {'gen','dom'}, dimensions={0} | all-to-all | bytes 65536 | tf_op jit(solution)/shard_map/all_to_all | solution.py:348
  116.5 0.7 shard_map.101
  (5 shorter events, 0.0 us)
Async XLA Ops:
  0.6 22.0 %collective-permute-start.12 = (bf16[128,1024]{1,0:T(8,128)(2,1)}, bf16[128,1024]{1,0:T(8,128)(2,1)S(1)}, u32[]{:S(2)}, u32[]{:S(2)}) collective-permute-start(bf16[128,1024]{1,0:T(8,128)(2,1)} %refs_4_.1), channel_id=1, source_target_pairs={{8,0},{0,8},{24,16},{16,24},{9,1},{1,9},{25,17},{17,25},{10,2},{2,... | collective-permute-start | bytes 786440 | tf_op jit(solution)/shard_map/ppermute | solution.py:42
  3.7 21.3 %collective-permute-start.13 = (bf16[128,1024]{1,0:T(8,128)(2,1)}, bf16[128,1024]{1,0:T(8,128)(2,1)S(1)}, u32[]{:S(2)}, u32[]{:S(2)}) collective-permute-start(bf16[128,1024]{1,0:T(8,128)(2,1)} %refs_4_.1), channel_id=1, source_target_pairs={{16,0},{24,8},{0,16},{8,24},{17,1},{25,9},{1,17},{9,25},{18,2},{26... | collective-permute-start | bytes 786440 | tf_op jit(solution)/shard_map/ppermute | solution.py:42
  5.2 20.8 %collective-permute-start.14 = (bf16[128,1024]{1,0:T(8,128)(2,1)}, bf16[128,1024]{1,0:T(8,128)(2,1)S(1)}, u32[]{:S(2)}, u32[]{:S(2)}) collective-permute-start(bf16[128,1024]{1,0:T(8,128)(2,1)} %refs_4_.1), channel_id=1, source_target_pairs={{24,0},{16,8},{8,16},{0,24},{25,1},{17,9},{9,17},{1,25},{26,2},{18... | collective-permute-start | bytes 786440 | tf_op jit(solution)/shard_map/ppermute | solution.py:42
  6.1 7.4 %collective-permute-start = (bf16[128,384]{1,0:T(8,128)(2,1)S(1)}, bf16[128,384]{1,0:T(8,128)(2,1)S(1)}, u32[]{:S(2)}, u32[]{:S(2)}) collective-permute-start(bf16[128,384]{1,0:T(8,128)(2,1)S(1)} %slice.6.refs_0_), channel_id=1, source_target_pairs={{6,0},{0,2},{2,4},{4,6},{7,1},{1,3},{3,5},{5,7},{14,8},{8,10},{10,... | collective-permute-start | bytes 294920 | tf_op jit(solution)/shard_map/ppermute | solution.py:42
  8.2 10.9 %collective-permute-start.1 = (bf16[128,384]{1,0:T(8,128)(2,1)S(1)}, bf16[128,384]{1,0:T(8,128)(2,1)S(1)}, u32[]{:S(2)}, u32[]{:S(2)}) collective-permute-start(bf16[128,384]{1,0:T(8,128)(2,1)S(1)} %slice.6.refs_0_), channel_id=1, source_target_pairs={{4,0},{6,2},{0,4},{2,6},{5,1},{7,3},{1,5},{3,7},{12,8},{14,10},{8,... | collective-permute-start | bytes 294920 | tf_op jit(solution)/shard_map/ppermute | solution.py:42
  13.5 5.5 %collective-permute-start.2 = (bf16[128,384]{1,0:T(8,128)(2,1)S(1)}, bf16[128,384]{1,0:T(8,128)(2,1)S(1)}, u32[]{:S(2)}, u32[]{:S(2)}) collective-permute-start(bf16[128,384]{1,0:T(8,128)(2,1)S(1)} %slice.6.refs_0_), channel_id=1, source_target_pairs={{2,0},{4,2},{6,4},{0,6},{3,1},{5,3},{7,5},{1,7},{10,8},{12,10},{14... | collective-permute-start | bytes 294920 | tf_op jit(solution)/shard_map/ppermute | solution.py:42
  15.0 0.9 copy-start
  15.9 0.7 copy-start.1
  16.6 0.7 copy-start.2
  17.4 0.7 copy-start.3
  18.0 0.7 copy-start.4
  19.5 27.3 %collective-permute-start.3 = (bf16[272,384]{1,0:T(8,128)(2,1)S(1)}, bf16[272,384]{1,0:T(8,128)(2,1)S(1)}, u32[]{:S(2)}, u32[]{:S(2)}) collective-permute-start(bf16[272,384]{1,0:T(8,128)(2,1)S(1)} %shard_map.96.refs_0_), channel_id=1, source_target_pairs={{8,0},{0,8},{24,16},{16,24},{9,1},{1,9},{25,17},{17,25},{10,2},{2,... | collective-permute-start | bytes 626696 | tf_op jit(solution)/shard_map/ppermute | solution.py:42
  22.0 9.0 %collective-permute-start.6 = (bf16[128,640]{1,0:T(8,128)(2,1)S(1)}, bf16[128,640]{1,0:T(8,128)(2,1)S(1)}, u32[]{:S(2)}, u32[]{:S(2)}) collective-permute-start(bf16[128,640]{1,0:T(8,128)(2,1)S(1)} %slice.7.refs_0_), channel_id=1, source_target_pairs={{6,0},{0,2},{2,4},{4,6},{7,1},{1,3},{3,5},{5,7},{14,8},{8,10},{10,... | collective-permute-start | bytes 491528 | tf_op jit(solution)/shard_map/ppermute | solution.py:42
  22.6 14.9 %collective-permute-start.7 = (bf16[128,640]{1,0:T(8,128)(2,1)S(1)}, bf16[128,640]{1,0:T(8,128)(2,1)S(1)}, u32[]{:S(2)}, u32[]{:S(2)}) collective-permute-start(bf16[128,640]{1,0:T(8,128)(2,1)S(1)} %slice.7.refs_0_), channel_id=1, source_target_pairs={{4,0},{6,2},{0,4},{2,6},{5,1},{7,3},{1,5},{3,7},{12,8},{14,10},{8,... | collective-permute-start | bytes 491528 | tf_op jit(solution)/shard_map/ppermute | solution.py:42
  24.9 20.7 %collective-permute-start.8 = (bf16[128,640]{1,0:T(8,128)(2,1)S(1)}, bf16[128,640]{1,0:T(8,128)(2,1)S(1)}, u32[]{:S(2)}, u32[]{:S(2)}) collective-permute-start(bf16[128,640]{1,0:T(8,128)(2,1)S(1)} %slice.7.refs_0_), channel_id=1, source_target_pairs={{2,0},{4,2},{6,4},{0,6},{3,1},{5,3},{7,5},{1,7},{10,8},{12,10},{14... | collective-permute-start | bytes 491528 | tf_op jit(solution)/shard_map/ppermute | solution.py:42
  26.7 21.6 %collective-permute-start.15 = (bf16[272,256]{1,0:T(8,128)(2,1)S(1)}, bf16[272,256]{1,0:T(8,128)(2,1)S(1)}, u32[]{:S(2)}, u32[]{:S(2)}) collective-permute-start(bf16[272,256]{1,0:T(8,128)(2,1)S(1)} %get-tuple-element.19), channel_id=1, source_target_pairs={{6,0},{0,2},{2,4},{4,6},{7,1},{1,3},{3,5},{5,7},{14,8},{8,10},{10,... | collective-permute-start | bytes 417800 | tf_op jit(solution)/shard_map/ppermute | solution.py:42
  31.0 18.8 %collective-permute-start.16 = (bf16[272,256]{1,0:T(8,128)(2,1)S(1)}, bf16[272,256]{1,0:T(8,128)(2,1)S(1)}, u32[]{:S(2)}, u32[]{:S(2)}) collective-permute-start(bf16[272,256]{1,0:T(8,128)(2,1)S(1)} %get-tuple-element.19), channel_id=1, source_target_pairs={{4,0},{6,2},{0,4},{2,6},{5,1},{7,3},{1,5},{3,7},{12,8},{14,10},{8,... | collective-permute-start | bytes 417800 | tf_op jit(solution)/shard_map/ppermute | solution.py:42
  37.6 13.8 %collective-permute-start.17 = (bf16[272,256]{1,0:T(8,128)(2,1)S(1)}, bf16[272,256]{1,0:T(8,128)(2,1)S(1)}, u32[]{:S(2)}, u32[]{:S(2)}) collective-permute-start(bf16[272,256]{1,0:T(8,128)(2,1)S(1)} %get-tuple-element.19), channel_id=1, source_target_pairs={{2,0},{4,2},{6,4},{0,6},{3,1},{5,3},{7,5},{1,7},{10,8},{12,10},{14... | collective-permute-start | bytes 417800 | tf_op jit(solution)/shard_map/ppermute | solution.py:42
  46.2 29.7 %collective-permute-start.9 = (bf16[272,640]{1,0:T(8,128)(2,1)S(1)}, bf16[272,640]{1,0:T(8,128)(2,1)S(1)}, u32[]{:S(2)}, u32[]{:S(2)}) collective-permute-start(bf16[272,640]{1,0:T(8,128)(2,1)S(1)} %shard_map.97.refs_4_), channel_id=1, source_target_pairs={{8,0},{0,8},{24,16},{16,24},{9,1},{1,9},{25,17},{17,25},{10,2},{2,... | collective-permute-start | bytes 1044488 | tf_op jit(solution)/shard_map/ppermute | solution.py:42
  46.8 30.6 %collective-permute-start.10 = (bf16[272,640]{1,0:T(8,128)(2,1)S(1)}, bf16[272,640]{1,0:T(8,128)(2,1)S(1)}, u32[]{:S(2)}, u32[]{:S(2)}) collective-permute-start(bf16[272,640]{1,0:T(8,128)(2,1)S(1)} %shard_map.97.refs_4_), channel_id=1, source_target_pairs={{16,0},{24,8},{0,16},{8,24},{17,1},{25,9},{1,17},{9,25},{18,2},{26... | collective-permute-start | bytes 1044488 | tf_op jit(solution)/shard_map/ppermute | solution.py:42
  48.3 29.1 %collective-permute-start.11 = (bf16[272,640]{1,0:T(8,128)(2,1)S(1)}, bf16[272,640]{1,0:T(8,128)(2,1)S(1)}, u32[]{:S(2)}, u32[]{:S(2)}) collective-permute-start(bf16[272,640]{1,0:T(8,128)(2,1)S(1)} %shard_map.97.refs_4_), channel_id=1, source_target_pairs={{24,0},{16,8},{8,16},{0,24},{25,1},{17,9},{9,17},{1,25},{26,2},{18... | collective-permute-start | bytes 1044488 | tf_op jit(solution)/shard_map/ppermute | solution.py:42
  49.8 23.9 %collective-permute-start.4 = (bf16[272,384]{1,0:T(8,128)(2,1)S(1)}, bf16[272,384]{1,0:T(8,128)(2,1)S(1)}, u32[]{:S(2)}, u32[]{:S(2)}) collective-permute-start(bf16[272,384]{1,0:T(8,128)(2,1)S(1)} %shard_map.96.refs_0_), channel_id=1, source_target_pairs={{16,0},{24,8},{0,16},{8,24},{17,1},{25,9},{1,17},{9,25},{18,2},{26... | collective-permute-start | bytes 626696 | tf_op jit(solution)/shard_map/ppermute | solution.py:42
  51.4 22.7 %collective-permute-start.5 = (bf16[272,384]{1,0:T(8,128)(2,1)S(1)}, bf16[272,384]{1,0:T(8,128)(2,1)S(1)}, u32[]{:S(2)}, u32[]{:S(2)}) collective-permute-start(bf16[272,384]{1,0:T(8,128)(2,1)S(1)} %shard_map.96.refs_0_), channel_id=1, source_target_pairs={{24,0},{16,8},{8,16},{0,24},{25,1},{17,9},{9,17},{1,25},{26,2},{18... | collective-permute-start | bytes 626696 | tf_op jit(solution)/shard_map/ppermute | solution.py:42
  73.7 18.0 %collective-permute-start.18 = (bf16[272,768]{1,0:T(8,128)(2,1)S(1)}, bf16[272,768]{1,0:T(8,128)(2,1)S(1)}, u32[]{:S(2)}, u32[]{:S(2)}) collective-permute-start(bf16[272,768]{1,0:T(8,128)(2,1)S(1)} %constant_dynamic-update-slice_fusion.refs_1_), channel_id=1, source_target_pairs={{8,0},{0,8},{24,16},{16,24},{9,1},{1,9},{25,17},{17,25},{10,2},{2,... | collective-permute-start | bytes 1253384 | tf_op jit(solution)/shard_map/ppermute | solution.py:42
  74.1 17.5 %collective-permute-start.19 = (bf16[272,768]{1,0:T(8,128)(2,1)S(1)}, bf16[272,768]{1,0:T(8,128)(2,1)S(1)}, u32[]{:S(2)}, u32[]{:S(2)}) collective-permute-start(bf16[272,768]{1,0:T(8,128)(2,1)S(1)} %constant_dynamic-update-slice_fusion.refs_1_), channel_id=1, source_target_pairs={{16,0},{24,8},{0,16},{8,24},{17,1},{25,9},{1,17},{9,25},{18,2},{26... | collective-permute-start | bytes 1253384 | tf_op jit(solution)/shard_map/ppermute | solution.py:42
  75.9 15.8 %collective-permute-start.20 = (bf16[272,768]{1,0:T(8,128)(2,1)S(1)}, bf16[272,768]{1,0:T(8,128)(2,1)S(1)}, u32[]{:S(2)}, u32[]{:S(2)}) collective-permute-start(bf16[272,768]{1,0:T(8,128)(2,1)S(1)} %constant_dynamic-update-slice_fusion.refs_1_), channel_id=1, source_target_pairs={{24,0},{16,8},{8,16},{0,24},{25,1},{17,9},{9,17},{1,25},{26,2},{18... | collective-permute-start | bytes 1253384 | tf_op jit(solution)/shard_map/ppermute | solution.py:42

commit v2 on v1

--- a/solution.py
+++ b/solution.py
@@ -34,13 +34,14 @@
     return list(zip(edges, edges[1:]))
 
 
+def moved(block, axis, k):
+    count = lax.axis_size(axis)
+    pairs = [(origin(axis, i, k, count), i) for i in range(count)]
+    return lax.ppermute(block, axis, pairs)
+
+
 def around(block, axis):
-    count = lax.axis_size(axis)
-    parts = [block]
-    for k in range(1, count):
-        pairs = [(origin(axis, i, k, count), i) for i in range(count)]
-        parts.append(lax.ppermute(block, axis, pairs))
-    return parts
+    return [block] + [moved(block, axis, k) for k in range(1, lax.axis_size(axis))]
 
 
 def pack_extents(doc):
@@ -329,12 +330,14 @@
     dom_parts = [(dom_rows, [lambda: dom_from(0) * dom_width])]
     if spans:
         span = dom_width // spans
-        received = around(dom_span[0], "dom")[1:]
+        received = [moved(dom_span[0], "dom", k) for k in range(2, dom_count)]
+        near = moved(dom_rows, "dom", 1)
+        dom_parts.append((near, [lambda: dom_from(1) * dom_width]))
         joined = jnp.concatenate(received, axis=1)
         for k, part in enumerate(around(joined, "gen")):
             places = [
                 lambda k=k, i=i: dom_from(i) * dom_width + gen_from(k) * span
-                for i in range(1, dom_count)
+                for i in range(2, dom_count)
             ]
             dom_parts.append((part, places))
     else:

time: 118 us -> 111 us (0.941)
  waiting for transfers between devices: 29.5 us -> 25.5 us
  starting transfers between devices: 39.5 us -> 37 us
    ppermute x21, waiting for transfers between devices: 29.5 us -> 25.5 us  [moved(): return lax.ppermute(block, axis, pairs)]
    ppermute x21, starting transfers between devices: 39.5 us -> 37 us  [moved(): return lax.ppermute(block, axis, pairs)]
    unnamed x12 -> x11, local copies, waits for them, and re-layouts: 3.77 us -> 3.79 us
  transfers between devices with their start and end apart: 21 -> 21, of which waited for: 4 -> 5; matrix products, arithmetic and copies ran while one was open for 2% -> 2% of each run, Pallas kernels for 14% -> 15%
where the time goes in v2:
time: 111 us; the launch traced here: 110 us
  starting transfers between devices  37 us (33%)
  Pallas kernels  31.2 us (28%)
  waiting for transfers between devices  25.5 us (23%)
  blocking collectives  9.94 us (9%)
  local copies, waits for them, and re-layouts  5.64 us (5%)
    ppermute x21, starting transfers between devices, moved(): return lax.ppermute(block, axis, pairs)  37 us
    pallas_call x2, Pallas kernels, stats(): pl.pallas_call(functools.partial(stats_kernel, tuple(pieces), buffers), g...  28.4 us
    ppermute x21, waiting for transfers between devices, moved(): return lax.ppermute(block, axis, pairs)  25.5 us
    all_to_all x1, blocking collectives, per_device(): gathered = lax.all_to_all(sent, ('gen', 'dom'), 0, 0)  9.94 us
    unnamed x11, local copies, waits for them, and re-layouts  3.79 us
  transfers between devices with their start and end apart: 21, of which 5 were waited for; matrix products, arithmetic and copies ran while one was open for 2% of the time, Pallas kernels for 15%

profile of v2, /device:TPU:0, one launch (start us, length us, event | category | flops | bytes accessed | tf_op | source)
XLA Modules:
  0.0 110.1 jit_solution(436628545870641223)
XLA Ops:
  0.6 3.0 %collective-permute-start.12 = (bf16[128,1024]{1,0:T(8,128)(2,1)}, bf16[128,1024]{1,0:T(8,128)(2,1)S(1)}, u32[]{:S(2)}, u32[]{:S(2)}) collective-permute-start(bf16[128,1024]{1,0:T(8,128)(2,1)} %refs_4_.1), channel_id=1, source_target_pairs={{8,0},{0,8},{24,16},{16,24},{9,1},{1,9},{25,17},{17,25},{10,2},{2,... | collective-permute-start | bytes 786440 | tf_op jit(solution)/shard_map/ppermute | solution.py:40
  3.7 1.5 %collective-permute-start.13 = (bf16[128,1024]{1,0:T(8,128)(2,1)}, bf16[128,1024]{1,0:T(8,128)(2,1)S(1)}, u32[]{:S(2)}, u32[]{:S(2)}) collective-permute-start(bf16[128,1024]{1,0:T(8,128)(2,1)} %refs_4_.1), channel_id=1, source_target_pairs={{16,0},{24,8},{0,16},{8,24},{17,1},{25,9},{1,17},{9,25},{18,2},{26... | collective-permute-start | bytes 786440 | tf_op jit(solution)/shard_map/ppermute | solution.py:40
  5.2 0.9 slice.6.refs_0_
  6.1 1.6 %collective-permute-start = (bf16[128,384]{1,0:T(8,128)(2,1)S(1)}, bf16[128,384]{1,0:T(8,128)(2,1)S(1)}, u32[]{:S(2)}, u32[]{:S(2)}) collective-permute-start(bf16[128,384]{1,0:T(8,128)(2,1)S(1)} %slice.6.refs_0_), channel_id=1, source_target_pairs={{6,0},{0,2},{2,4},{4,6},{7,1},{1,3},{3,5},{5,7},{14,8},{8,10},{10,... | collective-permute-start | bytes 294920 | tf_op jit(solution)/shard_map/ppermute | solution.py:40
  7.7 2.6 %collective-permute-start.1 = (bf16[128,384]{1,0:T(8,128)(2,1)S(1)}, bf16[128,384]{1,0:T(8,128)(2,1)S(1)}, u32[]{:S(2)}, u32[]{:S(2)}) collective-permute-start(bf16[128,384]{1,0:T(8,128)(2,1)S(1)} %slice.6.refs_0_), channel_id=1, source_target_pairs={{4,0},{6,2},{0,4},{2,6},{5,1},{7,3},{1,5},{3,7},{12,8},{14,10},{8,... | collective-permute-start | bytes 294920 | tf_op jit(solution)/shard_map/ppermute | solution.py:40
  10.3 1.3 %collective-permute-start.2 = (bf16[128,384]{1,0:T(8,128)(2,1)S(1)}, bf16[128,384]{1,0:T(8,128)(2,1)S(1)}, u32[]{:S(2)}, u32[]{:S(2)}) collective-permute-start(bf16[128,384]{1,0:T(8,128)(2,1)S(1)} %slice.6.refs_0_), channel_id=1, source_target_pairs={{2,0},{4,2},{6,4},{0,6},{3,1},{5,3},{7,5},{1,7},{10,8},{12,10},{14... | collective-permute-start | bytes 294920 | tf_op jit(solution)/shard_map/ppermute | solution.py:40
  11.7 2.0 %collective-permute-done.refs_1_ = bf16[128,384]{1,0:T(8,128)(2,1)S(1)} collective-permute-done((bf16[128,384]{1,0:T(8,128)(2,1)S(1)}, bf16[128,384]{1,0:T(8,128)(2,1)S(1)}, u32[]{:S(2)}, u32[]{:S(2)}) %collective-permute-start) | collective-permute-done | bytes 98336 | tf_op jit(solution)/shard_map/ppermute | solution.py:40
  13.7 0.3 collective-permute-start.14
  14.0 0.0 copy-start
  14.0 1.0 copy-done
  15.0 0.0 copy-start.1
  15.0 0.7 copy-done.1
  15.7 0.0 copy-start.2
  15.7 0.7 copy-done.2
  16.4 0.0 copy-start.3
  16.4 0.7 copy-done.3
  17.1 0.0 copy-start.4
  17.1 0.7 copy-done.4
  17.8 0.3 shard_map.95
  18.1 0.0 collective-permute-done.1.refs_2_
  18.1 0.0 collective-permute-done.2.refs_3_
  18.1 0.4 shard_map.96.refs_0_
  18.6 1.8 %collective-permute-start.3 = (bf16[272,384]{1,0:T(8,128)(2,1)S(1)}, bf16[272,384]{1,0:T(8,128)(2,1)S(1)}, u32[]{:S(2)}, u32[]{:S(2)}) collective-permute-start(bf16[272,384]{1,0:T(8,128)(2,1)S(1)} %shard_map.96.refs_0_), channel_id=1, source_target_pairs={{8,0},{0,8},{24,16},{16,24},{9,1},{1,9},{25,17},{17,25},{10,2},{2,... | collective-permute-start | bytes 626696 | tf_op jit(solution)/shard_map/ppermute | solution.py:40
  20.3 0.9 slice.7.refs_0_
  21.3 2.5 %collective-permute-start.6 = (bf16[128,640]{1,0:T(8,128)(2,1)S(1)}, bf16[128,640]{1,0:T(8,128)(2,1)S(1)}, u32[]{:S(2)}, u32[]{:S(2)}) collective-permute-start(bf16[128,640]{1,0:T(8,128)(2,1)S(1)} %slice.7.refs_0_), channel_id=1, source_target_pairs={{6,0},{0,2},{2,4},{4,6},{7,1},{1,3},{3,5},{5,7},{14,8},{8,10},{10,... | collective-permute-start | bytes 491528 | tf_op jit(solution)/shard_map/ppermute | solution.py:40
  23.7 0.0 collective-permute-done.12.refs_1_
  23.7 2.0 %collective-permute-start.7 = (bf16[128,640]{1,0:T(8,128)(2,1)S(1)}, bf16[128,640]{1,0:T(8,128)(2,1)S(1)}, u32[]{:S(2)}, u32[]{:S(2)}) collective-permute-start(bf16[128,640]{1,0:T(8,128)(2,1)S(1)} %slice.7.refs_0_), channel_id=1, source_target_pairs={{4,0},{6,2},{0,4},{2,6},{5,1},{7,3},{1,5},{3,7},{12,8},{14,10},{8,... | collective-permute-start | bytes 491528 | tf_op jit(solution)/shard_map/ppermute | solution.py:40
  25.7 0.0 collective-permute-done.13.refs_2_
  25.7 2.8 %collective-permute-start.8 = (bf16[128,640]{1,0:T(8,128)(2,1)S(1)}, bf16[128,640]{1,0:T(8,128)(2,1)S(1)}, u32[]{:S(2)}, u32[]{:S(2)}) collective-permute-start(bf16[128,640]{1,0:T(8,128)(2,1)S(1)} %slice.7.refs_0_), channel_id=1, source_target_pairs={{2,0},{4,2},{6,4},{0,6},{3,1},{5,3},{7,5},{1,7},{10,8},{12,10},{14... | collective-permute-start | bytes 491528 | tf_op jit(solution)/shard_map/ppermute | solution.py:40
  28.5 0.0 collective-permute-done.14.refs_3_
  28.6 0.7 shard_map.99
  29.3 0.1 collective-permute-start.16
  29.4 0.8 collective-permute-done.6.refs_1_
  30.2 2.8 %collective-permute-start.17 = (bf16[272,256]{1,0:T(8,128)(2,1)S(1)}, bf16[272,256]{1,0:T(8,128)(2,1)S(1)}, u32[]{:S(2)}, u32[]{:S(2)}) collective-permute-start(bf16[272,256]{1,0:T(8,128)(2,1)S(1)} %get-tuple-element.19), channel_id=1, source_target_pairs={{2,0},{4,2},{6,4},{0,6},{3,1},{5,3},{7,5},{1,7},{10,8},{12,10},{14... | collective-permute-start | bytes 417800 | tf_op jit(solution)/shard_map/ppermute | solution.py:40
  33.0 4.5 %collective-permute-done.7.refs_2_ = bf16[128,640]{1,0:T(8,128)(2,1)S(1)} collective-permute-done((bf16[128,640]{1,0:T(8,128)(2,1)S(1)}, bf16[128,640]{1,0:T(8,128)(2,1)S(1)}, u32[]{:S(2)}, u32[]{:S(2)}) %collective-permute-start.7) | collective-permute-done | bytes 163872 | tf_op jit(solution)/shard_map/ppermute | solution.py:40
  37.5 0.0 collective-permute-done.8.refs_3_
  37.5 0.6 shard_map.97.refs_4_
  38.1 0.1 collective-permute-start.9
  38.2 2.0 %collective-permute-start.10 = (bf16[272,640]{1,0:T(8,128)(2,1)S(1)}, bf16[272,640]{1,0:T(8,128)(2,1)S(1)}, u32[]{:S(2)}, u32[]{:S(2)}) collective-permute-start(bf16[272,640]{1,0:T(8,128)(2,1)S(1)} %shard_map.97.refs_4_), channel_id=1, source_target_pairs={{16,0},{24,8},{0,16},{8,24},{17,1},{25,9},{1,17},{9,25},{18,2},{26... | collective-permute-start | bytes 1044488 | tf_op jit(solution)/shard_map/ppermute | solution.py:40
  40.2 0.0 collective-permute-done.3.refs_1_
  40.2 1.4 %collective-permute-start.11 = (bf16[272,640]{1,0:T(8,128)(2,1)S(1)}, bf16[272,640]{1,0:T(8,128)(2,1)S(1)}, u32[]{:S(2)}, u32[]{:S(2)}) collective-permute-start(bf16[272,640]{1,0:T(8,128)(2,1)S(1)} %shard_map.97.refs_4_), channel_id=1, source_target_pairs={{24,0},{16,8},{8,16},{0,24},{25,1},{17,9},{9,17},{1,25},{26,2},{18... | collective-permute-start | bytes 1044488 | tf_op jit(solution)/shard_map/ppermute | solution.py:40
  41.7 2.2 %collective-permute-done.16 = bf16[272,256]{1,0:T(8,128)(2,1)S(1)} collective-permute-done((bf16[272,256]{1,0:T(8,128)(2,1)S(1)}, bf16[272,256]{1,0:T(8,128)(2,1)S(1)}, u32[]{:S(2)}, u32[]{:S(2)}) %collective-permute-start.16) | collective-permute-done | bytes 139296 | tf_op jit(solution)/shard_map/ppermute | solution.py:40
  43.9 1.5 %collective-permute-start.4 = (bf16[272,384]{1,0:T(8,128)(2,1)S(1)}, bf16[272,384]{1,0:T(8,128)(2,1)S(1)}, u32[]{:S(2)}, u32[]{:S(2)}) collective-permute-start(bf16[272,384]{1,0:T(8,128)(2,1)S(1)} %shard_map.96.refs_0_), channel_id=1, source_target_pairs={{16,0},{24,8},{0,16},{8,24},{17,1},{25,9},{1,17},{9,25},{18,2},{26... | collective-permute-start | bytes 626696 | tf_op jit(solution)/shard_map/ppermute | solution.py:40
  45.4 0.0 collective-permute-done.17
  45.4 0.6 collective-permute-start.5
  46.0 15.9 %collective-permute-done.4.refs_2_ = bf16[272,384]{1,0:T(8,128)(2,1)S(1)} collective-permute-done((bf16[272,384]{1,0:T(8,128)(2,1)S(1)}, bf16[272,384]{1,0:T(8,128)(2,1)S(1)}, u32[]{:S(2)}, u32[]{:S(2)}) %collective-permute-start.4) | collective-permute-done | bytes 208928 | tf_op jit(solution)/shard_map/ppermute | solution.py:40
  62.0 5.6 %collective-permute-start.15 = (bf16[272,1024]{1,0:T(8,128)(2,1)S(1)}, bf16[272,1024]{1,0:T(8,128)(2,1)S(1)}, u32[]{:S(2)}, u32[]{:S(2)}) collective-permute-start(bf16[272,1024]{1,0:T(8,128)(2,1)S(1)} %get-tuple-element.18.refs_0_), channel_id=1, source_target_pairs={{6,0},{0,2},{2,4},{4,6},{7,1},{1,3},{3,5},{5,7},{14,8},{8,10},{10,... | collective-permute-start | bytes 1671176 | tf_op jit(solution)/shard_map/ppermute | solution.py:40
  67.5 0.0 collective-permute-done.5.refs_3_
  67.5 0.4 collective-permute-start.18
  67.9 0.0 collective-permute-done.9.refs_5_
  67.9 0.9 collective-permute-start.19
  68.7 0.0 collective-permute-done.10.refs_6_
  68.7 2.3 %collective-permute-start.20 = (bf16[272,512]{1,0:T(8,128)(2,1)S(1)}, bf16[272,512]{1,0:T(8,128)(2,1)S(1)}, u32[]{:S(2)}, u32[]{:S(2)}) collective-permute-start(bf16[272,512]{1,0:T(8,128)(2,1)S(1)} %constant_dynamic-update-slice_fusion.refs_2_), channel_id=1, source_target_pairs={{24,0},{16,8},{8,16},{0,24},{25,1},{17,9},{9,17},{1,25},{26,2},{18... | collective-permute-start | bytes 835592 | tf_op jit(solution)/shard_map/ppermute | solution.py:40
  71.0 0.0 collective-permute-done.11.refs_7_
  71.0 14.2 %shard_map.98 = f32[4,2,128]{2,1,0:T(2,128)S(1)} custom-call(s32[272,128]{1,0:T(8,128)S(1)} %get-tuple-element.13.wanted_ref, bf16[272,512]{1,0:T(8,128)(2,1)S(1)} %get-tuple-element.14.live_ref, f32[1,4096]{1,0:T(1,128)S(1)} %get-tuple-element.15.gain_ref, bf16[4096,4096]{1,0:T(8,128)(2,1)} %head_ref.2, bf16[272,384]{1,0:T(8,128)(2,1)S(1)} %shard_map.96.refs_0_, ...), custom_call_target="tpu_custom_call" | custom-call | flops 9126805504 | bytes 35782656 | tf_op jit(solution)/shard_map/pallas_call | solution.py:239
  85.2 0.0 collective-permute-done.18.refs_3_
  85.2 0.0 collective-permute-done.19.refs_4_
  85.3 0.0 collective-permute-done.20.refs_5_
  85.3 0.0 collective-permute-done.15.refs_1_
  85.3 14.2 %shard_map.100 = f32[4,2,128]{2,1,0:T(2,128)S(1)} custom-call(s32[272,128]{1,0:T(8,128)S(1)} %get-tuple-element.13.wanted_ref, bf16[272,512]{1,0:T(8,128)(2,1)S(1)} %get-tuple-element.14.live_ref, f32[1,4096]{1,0:T(1,128)S(1)} %get-tuple-element.16.gain_ref, bf16[4096,4096]{1,0:T(8,128)(2,1)} %head_ref.3, bf16[272,1024]{1,0:T(8,128)(2,1)S(1)} %get-tuple-element.18.refs_0_, ...), custom_call_target="tpu_custom_call" | custom-call | flops 9126805504 | bytes 35782656 | tf_op jit(solution)/shard_map/pallas_call | solution.py:239
  99.6 9.9 %all_to_all.5.all_ref = f32[16,4,128]{2,1,0:T(4,128)S(1)} all-to-all(f32[16,4,128]{2,1,0:T(4,128)S(1)} %bitcast.11), channel_id=1, replica_groups=mesh['gen'=4,'dom'=4,'dp'=2] {'gen','dom'}, dimensions={0} | all-to-all | bytes 65536 | tf_op jit(solution)/shard_map/all_to_all | solution.py:351
  109.5 0.7 shard_map.101
  (4 shorter events, 0.0 us)
Async XLA Ops:
  0.6 23.1 %collective-permute-start.12 = (bf16[128,1024]{1,0:T(8,128)(2,1)}, bf16[128,1024]{1,0:T(8,128)(2,1)S(1)}, u32[]{:S(2)}, u32[]{:S(2)}) collective-permute-start(bf16[128,1024]{1,0:T(8,128)(2,1)} %refs_4_.1), channel_id=1, source_target_pairs={{8,0},{0,8},{24,16},{16,24},{9,1},{1,9},{25,17},{17,25},{10,2},{2,... | collective-permute-start | bytes 786440 | tf_op jit(solution)/shard_map/ppermute | solution.py:40
  3.7 22.0 %collective-permute-start.13 = (bf16[128,1024]{1,0:T(8,128)(2,1)}, bf16[128,1024]{1,0:T(8,128)(2,1)S(1)}, u32[]{:S(2)}, u32[]{:S(2)}) collective-permute-start(bf16[128,1024]{1,0:T(8,128)(2,1)} %refs_4_.1), channel_id=1, source_target_pairs={{16,0},{24,8},{0,16},{8,24},{17,1},{25,9},{1,17},{9,25},{18,2},{26... | collective-permute-start | bytes 786440 | tf_op jit(solution)/shard_map/ppermute | solution.py:40
  6.1 7.6 %collective-permute-start = (bf16[128,384]{1,0:T(8,128)(2,1)S(1)}, bf16[128,384]{1,0:T(8,128)(2,1)S(1)}, u32[]{:S(2)}, u32[]{:S(2)}) collective-permute-start(bf16[128,384]{1,0:T(8,128)(2,1)S(1)} %slice.6.refs_0_), channel_id=1, source_target_pairs={{6,0},{0,2},{2,4},{4,6},{7,1},{1,3},{3,5},{5,7},{14,8},{8,10},{10,... | collective-permute-start | bytes 294920 | tf_op jit(solution)/shard_map/ppermute | solution.py:40
  7.7 10.4 %collective-permute-start.1 = (bf16[128,384]{1,0:T(8,128)(2,1)S(1)}, bf16[128,384]{1,0:T(8,128)(2,1)S(1)}, u32[]{:S(2)}, u32[]{:S(2)}) collective-permute-start(bf16[128,384]{1,0:T(8,128)(2,1)S(1)} %slice.6.refs_0_), channel_id=1, source_target_pairs={{4,0},{6,2},{0,4},{2,6},{5,1},{7,3},{1,5},{3,7},{12,8},{14,10},{8,... | collective-permute-start | bytes 294920 | tf_op jit(solution)/shard_map/ppermute | solution.py:40
  10.3 7.8 %collective-permute-start.2 = (bf16[128,384]{1,0:T(8,128)(2,1)S(1)}, bf16[128,384]{1,0:T(8,128)(2,1)S(1)}, u32[]{:S(2)}, u32[]{:S(2)}) collective-permute-start(bf16[128,384]{1,0:T(8,128)(2,1)S(1)} %slice.6.refs_0_), channel_id=1, source_target_pairs={{2,0},{4,2},{6,4},{0,6},{3,1},{5,3},{7,5},{1,7},{10,8},{12,10},{14... | collective-permute-start | bytes 294920 | tf_op jit(solution)/shard_map/ppermute | solution.py:40
  13.7 14.8 %collective-permute-start.14 = (bf16[128,1024]{1,0:T(8,128)(2,1)}, bf16[128,1024]{1,0:T(8,128)(2,1)S(1)}, u32[]{:S(2)}, u32[]{:S(2)}) collective-permute-start(bf16[128,1024]{1,0:T(8,128)(2,1)} %refs_4_.1), channel_id=1, source_target_pairs={{24,0},{16,8},{8,16},{0,24},{25,1},{17,9},{9,17},{1,25},{26,2},{18... | collective-permute-start | bytes 786440 | tf_op jit(solution)/shard_map/ppermute | solution.py:40
  14.0 1.0 copy-start
  15.0 0.7 copy-start.1
  15.7 0.7 copy-start.2
  16.4 0.7 copy-start.3
  17.1 0.7 copy-start.4
  18.6 21.7 %collective-permute-start.3 = (bf16[272,384]{1,0:T(8,128)(2,1)S(1)}, bf16[272,384]{1,0:T(8,128)(2,1)S(1)}, u32[]{:S(2)}, u32[]{:S(2)}) collective-permute-start(bf16[272,384]{1,0:T(8,128)(2,1)S(1)} %shard_map.96.refs_0_), channel_id=1, source_target_pairs={{8,0},{0,8},{24,16},{16,24},{9,1},{1,9},{25,17},{17,25},{10,2},{2,... | collective-permute-start | bytes 626696 | tf_op jit(solution)/shard_map/ppermute | solution.py:40
  21.3 8.9 %collective-permute-start.6 = (bf16[128,640]{1,0:T(8,128)(2,1)S(1)}, bf16[128,640]{1,0:T(8,128)(2,1)S(1)}, u32[]{:S(2)}, u32[]{:S(2)}) collective-permute-start(bf16[128,640]{1,0:T(8,128)(2,1)S(1)} %slice.7.refs_0_), channel_id=1, source_target_pairs={{6,0},{0,2},{2,4},{4,6},{7,1},{1,3},{3,5},{5,7},{14,8},{8,10},{10,... | collective-permute-start | bytes 491528 | tf_op jit(solution)/shard_map/ppermute | solution.py:40
  23.7 13.8 %collective-permute-start.7 = (bf16[128,640]{1,0:T(8,128)(2,1)S(1)}, bf16[128,640]{1,0:T(8,128)(2,1)S(1)}, u32[]{:S(2)}, u32[]{:S(2)}) collective-permute-start(bf16[128,640]{1,0:T(8,128)(2,1)S(1)} %slice.7.refs_0_), channel_id=1, source_target_pairs={{4,0},{6,2},{0,4},{2,6},{5,1},{7,3},{1,5},{3,7},{12,8},{14,10},{8,... | collective-permute-start | bytes 491528 | tf_op jit(solution)/shard_map/ppermute | solution.py:40
  25.7 11.8 %collective-permute-start.8 = (bf16[128,640]{1,0:T(8,128)(2,1)S(1)}, bf16[128,640]{1,0:T(8,128)(2,1)S(1)}, u32[]{:S(2)}, u32[]{:S(2)}) collective-permute-start(bf16[128,640]{1,0:T(8,128)(2,1)S(1)} %slice.7.refs_0_), channel_id=1, source_target_pairs={{2,0},{4,2},{6,4},{0,6},{3,1},{5,3},{7,5},{1,7},{10,8},{12,10},{14... | collective-permute-start | bytes 491528 | tf_op jit(solution)/shard_map/ppermute | solution.py:40
  29.3 14.6 %collective-permute-start.16 = (bf16[272,256]{1,0:T(8,128)(2,1)S(1)}, bf16[272,256]{1,0:T(8,128)(2,1)S(1)}, u32[]{:S(2)}, u32[]{:S(2)}) collective-permute-start(bf16[272,256]{1,0:T(8,128)(2,1)S(1)} %get-tuple-element.19), channel_id=1, source_target_pairs={{4,0},{6,2},{0,4},{2,6},{5,1},{7,3},{1,5},{3,7},{12,8},{14,10},{8,... | collective-permute-start | bytes 417800 | tf_op jit(solution)/shard_map/ppermute | solution.py:40
  30.2 15.3 %collective-permute-start.17 = (bf16[272,256]{1,0:T(8,128)(2,1)S(1)}, bf16[272,256]{1,0:T(8,128)(2,1)S(1)}, u32[]{:S(2)}, u32[]{:S(2)}) collective-permute-start(bf16[272,256]{1,0:T(8,128)(2,1)S(1)} %get-tuple-element.19), channel_id=1, source_target_pairs={{2,0},{4,2},{6,4},{0,6},{3,1},{5,3},{7,5},{1,7},{10,8},{12,10},{14... | collective-permute-start | bytes 417800 | tf_op jit(solution)/shard_map/ppermute | solution.py:40
  38.1 29.8 %collective-permute-start.9 = (bf16[272,640]{1,0:T(8,128)(2,1)S(1)}, bf16[272,640]{1,0:T(8,128)(2,1)S(1)}, u32[]{:S(2)}, u32[]{:S(2)}) collective-permute-start(bf16[272,640]{1,0:T(8,128)(2,1)S(1)} %shard_map.97.refs_4_), channel_id=1, source_target_pairs={{8,0},{0,8},{24,16},{16,24},{9,1},{1,9},{25,17},{17,25},{10,2},{2,... | collective-permute-start | bytes 1044488 | tf_op jit(solution)/shard_map/ppermute | solution.py:40
  38.2 30.6 %collective-permute-start.10 = (bf16[272,640]{1,0:T(8,128)(2,1)S(1)}, bf16[272,640]{1,0:T(8,128)(2,1)S(1)}, u32[]{:S(2)}, u32[]{:S(2)}) collective-permute-start(bf16[272,640]{1,0:T(8,128)(2,1)S(1)} %shard_map.97.refs_4_), channel_id=1, source_target_pairs={{16,0},{24,8},{0,16},{8,24},{17,1},{25,9},{1,17},{9,25},{18,2},{26... | collective-permute-start | bytes 1044488 | tf_op jit(solution)/shard_map/ppermute | solution.py:40
  40.2 30.8 %collective-permute-start.11 = (bf16[272,640]{1,0:T(8,128)(2,1)S(1)}, bf16[272,640]{1,0:T(8,128)(2,1)S(1)}, u32[]{:S(2)}, u32[]{:S(2)}) collective-permute-start(bf16[272,640]{1,0:T(8,128)(2,1)S(1)} %shard_map.97.refs_4_), channel_id=1, source_target_pairs={{24,0},{16,8},{8,16},{0,24},{25,1},{17,9},{9,17},{1,25},{26,2},{18... | collective-permute-start | bytes 1044488 | tf_op jit(solution)/shard_map/ppermute | solution.py:40
  43.9 18.0 %collective-permute-start.4 = (bf16[272,384]{1,0:T(8,128)(2,1)S(1)}, bf16[272,384]{1,0:T(8,128)(2,1)S(1)}, u32[]{:S(2)}, u32[]{:S(2)}) collective-permute-start(bf16[272,384]{1,0:T(8,128)(2,1)S(1)} %shard_map.96.refs_0_), channel_id=1, source_target_pairs={{16,0},{24,8},{0,16},{8,24},{17,1},{25,9},{1,17},{9,25},{18,2},{26... | collective-permute-start | bytes 626696 | tf_op jit(solution)/shard_map/ppermute | solution.py:40
  45.4 22.1 %collective-permute-start.5 = (bf16[272,384]{1,0:T(8,128)(2,1)S(1)}, bf16[272,384]{1,0:T(8,128)(2,1)S(1)}, u32[]{:S(2)}, u32[]{:S(2)}) collective-permute-start(bf16[272,384]{1,0:T(8,128)(2,1)S(1)} %shard_map.96.refs_0_), channel_id=1, source_target_pairs={{24,0},{16,8},{8,16},{0,24},{25,1},{17,9},{9,17},{1,25},{26,2},{18... | collective-permute-start | bytes 626696 | tf_op jit(solution)/shard_map/ppermute | solution.py:40
  62.0 23.3 %collective-permute-start.15 = (bf16[272,1024]{1,0:T(8,128)(2,1)S(1)}, bf16[272,1024]{1,0:T(8,128)(2,1)S(1)}, u32[]{:S(2)}, u32[]{:S(2)}) collective-permute-start(bf16[272,1024]{1,0:T(8,128)(2,1)S(1)} %get-tuple-element.18.refs_0_), channel_id=1, source_target_pairs={{6,0},{0,2},{2,4},{4,6},{7,1},{1,3},{3,5},{5,7},{14,8},{8,10},{10,... | collective-permute-start | bytes 1671176 | tf_op jit(solution)/shard_map/ppermute | solution.py:40
  67.5 17.7 %collective-permute-start.18 = (bf16[272,512]{1,0:T(8,128)(2,1)S(1)}, bf16[272,512]{1,0:T(8,128)(2,1)S(1)}, u32[]{:S(2)}, u32[]{:S(2)}) collective-permute-start(bf16[272,512]{1,0:T(8,128)(2,1)S(1)} %constant_dynamic-update-slice_fusion.refs_2_), channel_id=1, source_target_pairs={{8,0},{0,8},{24,16},{16,24},{9,1},{1,9},{25,17},{17,25},{10,2},{2,... | collective-permute-start | bytes 835592 | tf_op jit(solution)/shard_map/ppermute | solution.py:40
  67.9 17.4 %collective-permute-start.19 = (bf16[272,512]{1,0:T(8,128)(2,1)S(1)}, bf16[272,512]{1,0:T(8,128)(2,1)S(1)}, u32[]{:S(2)}, u32[]{:S(2)}) collective-permute-start(bf16[272,512]{1,0:T(8,128)(2,1)S(1)} %constant_dynamic-update-slice_fusion.refs_2_), channel_id=1, source_target_pairs={{16,0},{24,8},{0,16},{8,24},{17,1},{25,9},{1,17},{9,25},{18,2},{26... | collective-permute-start | bytes 835592 | tf_op jit(solution)/shard_map/ppermute | solution.py:40
  68.7 16.5 %collective-permute-start.20 = (bf16[272,512]{1,0:T(8,128)(2,1)S(1)}, bf16[272,512]{1,0:T(8,128)(2,1)S(1)}, u32[]{:S(2)}, u32[]{:S(2)}) collective-permute-start(bf16[272,512]{1,0:T(8,128)(2,1)S(1)} %constant_dynamic-update-slice_fusion.refs_2_), channel_id=1, source_target_pairs={{24,0},{16,8},{8,16},{0,24},{25,1},{17,9},{9,17},{1,25},{26,2},{18... | collective-permute-start | bytes 835592 | tf_op jit(solution)/shard_map/ppermute | solution.py:40

commit v3 on v2

--- a/solution.py
+++ b/solution.py
@@ -193,10 +193,12 @@
 
     @pl.when(j == 0)
     def _():
-        sums = jnp.zeros((slots, 1), jnp.float32)
+        squares = jnp.zeros((slots, 128), jnp.float32)
         for part_ref in part_refs:
-            values = part_ref[...].astype(jnp.float32)
-            sums = sums + jnp.sum(values * values, axis=1, keepdims=True)
+            for start in range(0, part_ref.shape[1], 128):
+                values = part_ref[:, start : start + 128].astype(jnp.float32)
+                squares = squares + values * values
+        sums = jnp.sum(squares, axis=1, keepdims=True)
         scale = lax.rsqrt(sums / width + EPS)
         for part, start, extent, place in pieces:
             at = pl.ds(pl.multiple_of(place(), 128), extent)

time: 111 us -> 110 us (level)
  no operation moved by 1% of the time
where the time goes in v3:
time: 110 us
  starting transfers between devices  37 us (34%)
  Pallas kernels  31.1 us (28%)
  waiting for transfers between devices  25.5 us (23%)
  blocking collectives  9.94 us (9%)
  local copies, waits for them, and re-layouts  5.64 us (5%)
    ppermute x21, starting transfers between devices, moved(): return lax.ppermute(block, axis, pairs)  37 us
    pallas_call x2, Pallas kernels, stats(): pl.pallas_call(functools.partial(stats_kernel, tuple(pieces), buffers), g...  28.3 us
    ppermute x21, waiting for transfers between devices, moved(): return lax.ppermute(block, axis, pairs)  25.5 us
    all_to_all x1, blocking collectives, per_device(): gathered = lax.all_to_all(sent, ('gen', 'dom'), 0, 0)  9.94 us
    unnamed x11, local copies, waits for them, and re-layouts  3.79 us
  transfers between devices with their start and end apart: 21, of which 5 were waited for; matrix products, arithmetic and copies ran while one was open for 2% of the time, Pallas kernels for 15%

profile of v3, /device:TPU:0, one launch (start us, length us, event | category | flops | bytes accessed | tf_op | source)
XLA Modules:
  0.0 110.0 jit_solution(16409020600827483560)
XLA Ops:
  0.6 3.0 %collective-permute-start.12 = (bf16[128,1024]{1,0:T(8,128)(2,1)}, bf16[128,1024]{1,0:T(8,128)(2,1)S(1)}, u32[]{:S(2)}, u32[]{:S(2)}) collective-permute-start(bf16[128,1024]{1,0:T(8,128)(2,1)} %refs_4_.1), channel_id=1, source_target_pairs={{8,0},{0,8},{24,16},{16,24},{9,1},{1,9},{25,17},{17,25},{10,2},{2,... | collective-permute-start | bytes 786440 | tf_op jit(solution)/shard_map/ppermute | solution.py:40
  3.7 1.5 %collective-permute-start.13 = (bf16[128,1024]{1,0:T(8,128)(2,1)}, bf16[128,1024]{1,0:T(8,128)(2,1)S(1)}, u32[]{:S(2)}, u32[]{:S(2)}) collective-permute-start(bf16[128,1024]{1,0:T(8,128)(2,1)} %refs_4_.1), channel_id=1, source_target_pairs={{16,0},{24,8},{0,16},{8,24},{17,1},{25,9},{1,17},{9,25},{18,2},{26... | collective-permute-start | bytes 786440 | tf_op jit(solution)/shard_map/ppermute | solution.py:40
  5.2 0.9 slice.6.refs_0_
  6.1 1.6 %collective-permute-start = (bf16[128,384]{1,0:T(8,128)(2,1)S(1)}, bf16[128,384]{1,0:T(8,128)(2,1)S(1)}, u32[]{:S(2)}, u32[]{:S(2)}) collective-permute-start(bf16[128,384]{1,0:T(8,128)(2,1)S(1)} %slice.6.refs_0_), channel_id=1, source_target_pairs={{6,0},{0,2},{2,4},{4,6},{7,1},{1,3},{3,5},{5,7},{14,8},{8,10},{10,... | collective-permute-start | bytes 294920 | tf_op jit(solution)/shard_map/ppermute | solution.py:40
  7.7 2.6 %collective-permute-start.1 = (bf16[128,384]{1,0:T(8,128)(2,1)S(1)}, bf16[128,384]{1,0:T(8,128)(2,1)S(1)}, u32[]{:S(2)}, u32[]{:S(2)}) collective-permute-start(bf16[128,384]{1,0:T(8,128)(2,1)S(1)} %slice.6.refs_0_), channel_id=1, source_target_pairs={{4,0},{6,2},{0,4},{2,6},{5,1},{7,3},{1,5},{3,7},{12,8},{14,10},{8,... | collective-permute-start | bytes 294920 | tf_op jit(solution)/shard_map/ppermute | solution.py:40
  10.3 1.3 %collective-permute-start.2 = (bf16[128,384]{1,0:T(8,128)(2,1)S(1)}, bf16[128,384]{1,0:T(8,128)(2,1)S(1)}, u32[]{:S(2)}, u32[]{:S(2)}) collective-permute-start(bf16[128,384]{1,0:T(8,128)(2,1)S(1)} %slice.6.refs_0_), channel_id=1, source_target_pairs={{2,0},{4,2},{6,4},{0,6},{3,1},{5,3},{7,5},{1,7},{10,8},{12,10},{14... | collective-permute-start | bytes 294920 | tf_op jit(solution)/shard_map/ppermute | solution.py:40
  11.7 2.0 %collective-permute-done.refs_1_ = bf16[128,384]{1,0:T(8,128)(2,1)S(1)} collective-permute-done((bf16[128,384]{1,0:T(8,128)(2,1)S(1)}, bf16[128,384]{1,0:T(8,128)(2,1)S(1)}, u32[]{:S(2)}, u32[]{:S(2)}) %collective-permute-start) | collective-permute-done | bytes 98336 | tf_op jit(solution)/shard_map/ppermute | solution.py:40
  13.7 0.3 collective-permute-start.14
  14.0 0.0 copy-start
  14.0 1.0 copy-done
  15.0 0.0 copy-start.1
  15.0 0.7 copy-done.1
  15.7 0.0 copy-start.2
  15.7 0.7 copy-done.2
  16.4 0.0 copy-start.3
  16.4 0.7 copy-done.3
  17.1 0.0 copy-start.4
  17.1 0.7 copy-done.4
  17.8 0.3 shard_map.95
  18.1 0.0 collective-permute-done.1.refs_2_
  18.1 0.0 collective-permute-done.2.refs_3_
  18.1 0.4 shard_map.96.refs_0_
  18.6 1.8 %collective-permute-start.3 = (bf16[272,384]{1,0:T(8,128)(2,1)S(1)}, bf16[272,384]{1,0:T(8,128)(2,1)S(1)}, u32[]{:S(2)}, u32[]{:S(2)}) collective-permute-start(bf16[272,384]{1,0:T(8,128)(2,1)S(1)} %shard_map.96.refs_0_), channel_id=1, source_target_pairs={{8,0},{0,8},{24,16},{16,24},{9,1},{1,9},{25,17},{17,25},{10,2},{2,... | collective-permute-start | bytes 626696 | tf_op jit(solution)/shard_map/ppermute | solution.py:40
  20.3 0.9 slice.7.refs_0_
  21.3 2.5 %collective-permute-start.6 = (bf16[128,640]{1,0:T(8,128)(2,1)S(1)}, bf16[128,640]{1,0:T(8,128)(2,1)S(1)}, u32[]{:S(2)}, u32[]{:S(2)}) collective-permute-start(bf16[128,640]{1,0:T(8,128)(2,1)S(1)} %slice.7.refs_0_), channel_id=1, source_target_pairs={{6,0},{0,2},{2,4},{4,6},{7,1},{1,3},{3,5},{5,7},{14,8},{8,10},{10,... | collective-permute-start | bytes 491528 | tf_op jit(solution)/shard_map/ppermute | solution.py:40
  23.7 0.0 collective-permute-done.12.refs_1_
  23.7 2.0 %collective-permute-start.7 = (bf16[128,640]{1,0:T(8,128)(2,1)S(1)}, bf16[128,640]{1,0:T(8,128)(2,1)S(1)}, u32[]{:S(2)}, u32[]{:S(2)}) collective-permute-start(bf16[128,640]{1,0:T(8,128)(2,1)S(1)} %slice.7.refs_0_), channel_id=1, source_target_pairs={{4,0},{6,2},{0,4},{2,6},{5,1},{7,3},{1,5},{3,7},{12,8},{14,10},{8,... | collective-permute-start | bytes 491528 | tf_op jit(solution)/shard_map/ppermute | solution.py:40
  25.7 0.0 collective-permute-done.13.refs_2_
  25.7 2.8 %collective-permute-start.8 = (bf16[128,640]{1,0:T(8,128)(2,1)S(1)}, bf16[128,640]{1,0:T(8,128)(2,1)S(1)}, u32[]{:S(2)}, u32[]{:S(2)}) collective-permute-start(bf16[128,640]{1,0:T(8,128)(2,1)S(1)} %slice.7.refs_0_), channel_id=1, source_target_pairs={{2,0},{4,2},{6,4},{0,6},{3,1},{5,3},{7,5},{1,7},{10,8},{12,10},{14... | collective-permute-start | bytes 491528 | tf_op jit(solution)/shard_map/ppermute | solution.py:40
  28.5 0.0 collective-permute-done.14.refs_3_
  28.6 0.7 shard_map.99
  29.3 0.1 collective-permute-start.16
  29.4 0.8 collective-permute-done.6.refs_1_
  30.2 2.8 %collective-permute-start.17 = (bf16[272,256]{1,0:T(8,128)(2,1)S(1)}, bf16[272,256]{1,0:T(8,128)(2,1)S(1)}, u32[]{:S(2)}, u32[]{:S(2)}) collective-permute-start(bf16[272,256]{1,0:T(8,128)(2,1)S(1)} %get-tuple-element.19), channel_id=1, source_target_pairs={{2,0},{4,2},{6,4},{0,6},{3,1},{5,3},{7,5},{1,7},{10,8},{12,10},{14... | collective-permute-start | bytes 417800 | tf_op jit(solution)/shard_map/ppermute | solution.py:40
  33.0 4.5 %collective-permute-done.7.refs_2_ = bf16[128,640]{1,0:T(8,128)(2,1)S(1)} collective-permute-done((bf16[128,640]{1,0:T(8,128)(2,1)S(1)}, bf16[128,640]{1,0:T(8,128)(2,1)S(1)}, u32[]{:S(2)}, u32[]{:S(2)}) %collective-permute-start.7) | collective-permute-done | bytes 163872 | tf_op jit(solution)/shard_map/ppermute | solution.py:40
  37.5 0.0 collective-permute-done.8.refs_3_
  37.5 0.6 shard_map.97.refs_4_
  38.1 0.1 collective-permute-start.9
  38.2 2.0 %collective-permute-start.10 = (bf16[272,640]{1,0:T(8,128)(2,1)S(1)}, bf16[272,640]{1,0:T(8,128)(2,1)S(1)}, u32[]{:S(2)}, u32[]{:S(2)}) collective-permute-start(bf16[272,640]{1,0:T(8,128)(2,1)S(1)} %shard_map.97.refs_4_), channel_id=1, source_target_pairs={{16,0},{24,8},{0,16},{8,24},{17,1},{25,9},{1,17},{9,25},{18,2},{26... | collective-permute-start | bytes 1044488 | tf_op jit(solution)/shard_map/ppermute | solution.py:40
  40.2 0.0 collective-permute-done.3.refs_1_
  40.2 1.4 %collective-permute-start.11 = (bf16[272,640]{1,0:T(8,128)(2,1)S(1)}, bf16[272,640]{1,0:T(8,128)(2,1)S(1)}, u32[]{:S(2)}, u32[]{:S(2)}) collective-permute-start(bf16[272,640]{1,0:T(8,128)(2,1)S(1)} %shard_map.97.refs_4_), channel_id=1, source_target_pairs={{24,0},{16,8},{8,16},{0,24},{25,1},{17,9},{9,17},{1,25},{26,2},{18... | collective-permute-start | bytes 1044488 | tf_op jit(solution)/shard_map/ppermute | solution.py:40
  41.7 2.2 %collective-permute-done.16 = bf16[272,256]{1,0:T(8,128)(2,1)S(1)} collective-permute-done((bf16[272,256]{1,0:T(8,128)(2,1)S(1)}, bf16[272,256]{1,0:T(8,128)(2,1)S(1)}, u32[]{:S(2)}, u32[]{:S(2)}) %collective-permute-start.16) | collective-permute-done | bytes 139296 | tf_op jit(solution)/shard_map/ppermute | solution.py:40
  43.9 1.5 %collective-permute-start.4 = (bf16[272,384]{1,0:T(8,128)(2,1)S(1)}, bf16[272,384]{1,0:T(8,128)(2,1)S(1)}, u32[]{:S(2)}, u32[]{:S(2)}) collective-permute-start(bf16[272,384]{1,0:T(8,128)(2,1)S(1)} %shard_map.96.refs_0_), channel_id=1, source_target_pairs={{16,0},{24,8},{0,16},{8,24},{17,1},{25,9},{1,17},{9,25},{18,2},{26... | collective-permute-start | bytes 626696 | tf_op jit(solution)/shard_map/ppermute | solution.py:40
  45.4 0.0 collective-permute-done.17
  45.4 0.6 collective-permute-start.5
  46.0 15.9 %collective-permute-done.4.refs_2_ = bf16[272,384]{1,0:T(8,128)(2,1)S(1)} collective-permute-done((bf16[272,384]{1,0:T(8,128)(2,1)S(1)}, bf16[272,384]{1,0:T(8,128)(2,1)S(1)}, u32[]{:S(2)}, u32[]{:S(2)}) %collective-permute-start.4) | collective-permute-done | bytes 208928 | tf_op jit(solution)/shard_map/ppermute | solution.py:40
  62.0 5.6 %collective-permute-start.15 = (bf16[272,1024]{1,0:T(8,128)(2,1)S(1)}, bf16[272,1024]{1,0:T(8,128)(2,1)S(1)}, u32[]{:S(2)}, u32[]{:S(2)}) collective-permute-start(bf16[272,1024]{1,0:T(8,128)(2,1)S(1)} %get-tuple-element.18.refs_0_), channel_id=1, source_target_pairs={{6,0},{0,2},{2,4},{4,6},{7,1},{1,3},{3,5},{5,7},{14,8},{8,10},{10,... | collective-permute-start | bytes 1671176 | tf_op jit(solution)/shard_map/ppermute | solution.py:40
  67.5 0.0 collective-permute-done.5.refs_3_
  67.5 0.4 collective-permute-start.18
  67.9 0.0 collective-permute-done.9.refs_5_
  67.9 0.9 collective-permute-start.19
  68.7 0.0 collective-permute-done.10.refs_6_
  68.7 2.3 %collective-permute-start.20 = (bf16[272,512]{1,0:T(8,128)(2,1)S(1)}, bf16[272,512]{1,0:T(8,128)(2,1)S(1)}, u32[]{:S(2)}, u32[]{:S(2)}) collective-permute-start(bf16[272,512]{1,0:T(8,128)(2,1)S(1)} %constant_dynamic-update-slice_fusion.refs_2_), channel_id=1, source_target_pairs={{24,0},{16,8},{8,16},{0,24},{25,1},{17,9},{9,17},{1,25},{26,2},{18... | collective-permute-start | bytes 835592 | tf_op jit(solution)/shard_map/ppermute | solution.py:40
  71.0 0.0 collective-permute-done.11.refs_7_
  71.0 14.1 %shard_map.98 = f32[4,2,128]{2,1,0:T(2,128)S(1)} custom-call(s32[272,128]{1,0:T(8,128)S(1)} %get-tuple-element.13.wanted_ref, bf16[272,512]{1,0:T(8,128)(2,1)S(1)} %get-tuple-element.14.live_ref, f32[1,4096]{1,0:T(1,128)S(1)} %get-tuple-element.15.gain_ref, bf16[4096,4096]{1,0:T(8,128)(2,1)} %head_ref.2, bf16[272,384]{1,0:T(8,128)(2,1)S(1)} %shard_map.96.refs_0_, ...), custom_call_target="tpu_custom_call" | custom-call | flops 9126805504 | bytes 35782656 | tf_op jit(solution)/shard_map/pallas_call | solution.py:241
  85.2 0.0 collective-permute-done.18.refs_3_
  85.2 0.0 collective-permute-done.19.refs_4_
  85.2 0.0 collective-permute-done.20.refs_5_
  85.2 0.0 collective-permute-done.15.refs_1_
  85.2 14.2 %shard_map.100 = f32[4,2,128]{2,1,0:T(2,128)S(1)} custom-call(s32[272,128]{1,0:T(8,128)S(1)} %get-tuple-element.13.wanted_ref, bf16[272,512]{1,0:T(8,128)(2,1)S(1)} %get-tuple-element.14.live_ref, f32[1,4096]{1,0:T(1,128)S(1)} %get-tuple-element.16.gain_ref, bf16[4096,4096]{1,0:T(8,128)(2,1)} %head_ref.3, bf16[272,1024]{1,0:T(8,128)(2,1)S(1)} %get-tuple-element.18.refs_0_, ...), custom_call_target="tpu_custom_call" | custom-call | flops 9126805504 | bytes 35782656 | tf_op jit(solution)/shard_map/pallas_call | solution.py:241
  99.4 9.9 %all_to_all.5.all_ref = f32[16,4,128]{2,1,0:T(4,128)S(1)} all-to-all(f32[16,4,128]{2,1,0:T(4,128)S(1)} %bitcast.11), channel_id=1, replica_groups=mesh['gen'=4,'dom'=4,'dp'=2] {'gen','dom'}, dimensions={0} | all-to-all | bytes 65536 | tf_op jit(solution)/shard_map/all_to_all | solution.py:353
  109.4 0.7 shard_map.101
  (4 shorter events, 0.0 us)
Async XLA Ops:
  0.6 23.1 %collective-permute-start.12 = (bf16[128,1024]{1,0:T(8,128)(2,1)}, bf16[128,1024]{1,0:T(8,128)(2,1)S(1)}, u32[]{:S(2)}, u32[]{:S(2)}) collective-permute-start(bf16[128,1024]{1,0:T(8,128)(2,1)} %refs_4_.1), channel_id=1, source_target_pairs={{8,0},{0,8},{24,16},{16,24},{9,1},{1,9},{25,17},{17,25},{10,2},{2,... | collective-permute-start | bytes 786440 | tf_op jit(solution)/shard_map/ppermute | solution.py:40
  3.7 22.0 %collective-permute-start.13 = (bf16[128,1024]{1,0:T(8,128)(2,1)}, bf16[128,1024]{1,0:T(8,128)(2,1)S(1)}, u32[]{:S(2)}, u32[]{:S(2)}) collective-permute-start(bf16[128,1024]{1,0:T(8,128)(2,1)} %refs_4_.1), channel_id=1, source_target_pairs={{16,0},{24,8},{0,16},{8,24},{17,1},{25,9},{1,17},{9,25},{18,2},{26... | collective-permute-start | bytes 786440 | tf_op jit(solution)/shard_map/ppermute | solution.py:40
  6.1 7.6 %collective-permute-start = (bf16[128,384]{1,0:T(8,128)(2,1)S(1)}, bf16[128,384]{1,0:T(8,128)(2,1)S(1)}, u32[]{:S(2)}, u32[]{:S(2)}) collective-permute-start(bf16[128,384]{1,0:T(8,128)(2,1)S(1)} %slice.6.refs_0_), channel_id=1, source_target_pairs={{6,0},{0,2},{2,4},{4,6},{7,1},{1,3},{3,5},{5,7},{14,8},{8,10},{10,... | collective-permute-start | bytes 294920 | tf_op jit(solution)/shard_map/ppermute | solution.py:40
  7.7 10.4 %collective-permute-start.1 = (bf16[128,384]{1,0:T(8,128)(2,1)S(1)}, bf16[128,384]{1,0:T(8,128)(2,1)S(1)}, u32[]{:S(2)}, u32[]{:S(2)}) collective-permute-start(bf16[128,384]{1,0:T(8,128)(2,1)S(1)} %slice.6.refs_0_), channel_id=1, source_target_pairs={{4,0},{6,2},{0,4},{2,6},{5,1},{7,3},{1,5},{3,7},{12,8},{14,10},{8,... | collective-permute-start | bytes 294920 | tf_op jit(solution)/shard_map/ppermute | solution.py:40
  10.3 7.8 %collective-permute-start.2 = (bf16[128,384]{1,0:T(8,128)(2,1)S(1)}, bf16[128,384]{1,0:T(8,128)(2,1)S(1)}, u32[]{:S(2)}, u32[]{:S(2)}) collective-permute-start(bf16[128,384]{1,0:T(8,128)(2,1)S(1)} %slice.6.refs_0_), channel_id=1, source_target_pairs={{2,0},{4,2},{6,4},{0,6},{3,1},{5,3},{7,5},{1,7},{10,8},{12,10},{14... | collective-permute-start | bytes 294920 | tf_op jit(solution)/shard_map/ppermute | solution.py:40
  13.7 14.8 %collective-permute-start.14 = (bf16[128,1024]{1,0:T(8,128)(2,1)}, bf16[128,1024]{1,0:T(8,128)(2,1)S(1)}, u32[]{:S(2)}, u32[]{:S(2)}) collective-permute-start(bf16[128,1024]{1,0:T(8,128)(2,1)} %refs_4_.1), channel_id=1, source_target_pairs={{24,0},{16,8},{8,16},{0,24},{25,1},{17,9},{9,17},{1,25},{26,2},{18... | collective-permute-start | bytes 786440 | tf_op jit(solution)/shard_map/ppermute | solution.py:40
  14.0 1.0 copy-start
  15.0 0.7 copy-start.1
  15.7 0.7 copy-start.2
  16.4 0.7 copy-start.3
  17.1 0.7 copy-start.4
  18.6 21.7 %collective-permute-start.3 = (bf16[272,384]{1,0:T(8,128)(2,1)S(1)}, bf16[272,384]{1,0:T(8,128)(2,1)S(1)}, u32[]{:S(2)}, u32[]{:S(2)}) collective-permute-start(bf16[272,384]{1,0:T(8,128)(2,1)S(1)} %shard_map.96.refs_0_), channel_id=1, source_target_pairs={{8,0},{0,8},{24,16},{16,24},{9,1},{1,9},{25,17},{17,25},{10,2},{2,... | collective-permute-start | bytes 626696 | tf_op jit(solution)/shard_map/ppermute | solution.py:40
  21.3 8.9 %collective-permute-start.6 = (bf16[128,640]{1,0:T(8,128)(2,1)S(1)}, bf16[128,640]{1,0:T(8,128)(2,1)S(1)}, u32[]{:S(2)}, u32[]{:S(2)}) collective-permute-start(bf16[128,640]{1,0:T(8,128)(2,1)S(1)} %slice.7.refs_0_), channel_id=1, source_target_pairs={{6,0},{0,2},{2,4},{4,6},{7,1},{1,3},{3,5},{5,7},{14,8},{8,10},{10,... | collective-permute-start | bytes 491528 | tf_op jit(solution)/shard_map/ppermute | solution.py:40
  23.7 13.8 %collective-permute-start.7 = (bf16[128,640]{1,0:T(8,128)(2,1)S(1)}, bf16[128,640]{1,0:T(8,128)(2,1)S(1)}, u32[]{:S(2)}, u32[]{:S(2)}) collective-permute-start(bf16[128,640]{1,0:T(8,128)(2,1)S(1)} %slice.7.refs_0_), channel_id=1, source_target_pairs={{4,0},{6,2},{0,4},{2,6},{5,1},{7,3},{1,5},{3,7},{12,8},{14,10},{8,... | collective-permute-start | bytes 491528 | tf_op jit(solution)/shard_map/ppermute | solution.py:40
  25.7 11.8 %collective-permute-start.8 = (bf16[128,640]{1,0:T(8,128)(2,1)S(1)}, bf16[128,640]{1,0:T(8,128)(2,1)S(1)}, u32[]{:S(2)}, u32[]{:S(2)}) collective-permute-start(bf16[128,640]{1,0:T(8,128)(2,1)S(1)} %slice.7.refs_0_), channel_id=1, source_target_pairs={{2,0},{4,2},{6,4},{0,6},{3,1},{5,3},{7,5},{1,7},{10,8},{12,10},{14... | collective-permute-start | bytes 491528 | tf_op jit(solution)/shard_map/ppermute | solution.py:40
  29.3 14.6 %collective-permute-start.16 = (bf16[272,256]{1,0:T(8,128)(2,1)S(1)}, bf16[272,256]{1,0:T(8,128)(2,1)S(1)}, u32[]{:S(2)}, u32[]{:S(2)}) collective-permute-start(bf16[272,256]{1,0:T(8,128)(2,1)S(1)} %get-tuple-element.19), channel_id=1, source_target_pairs={{4,0},{6,2},{0,4},{2,6},{5,1},{7,3},{1,5},{3,7},{12,8},{14,10},{8,... | collective-permute-start | bytes 417800 | tf_op jit(solution)/shard_map/ppermute | solution.py:40
  30.2 15.3 %collective-permute-start.17 = (bf16[272,256]{1,0:T(8,128)(2,1)S(1)}, bf16[272,256]{1,0:T(8,128)(2,1)S(1)}, u32[]{:S(2)}, u32[]{:S(2)}) collective-permute-start(bf16[272,256]{1,0:T(8,128)(2,1)S(1)} %get-tuple-element.19), channel_id=1, source_target_pairs={{2,0},{4,2},{6,4},{0,6},{3,1},{5,3},{7,5},{1,7},{10,8},{12,10},{14... | collective-permute-start | bytes 417800 | tf_op jit(solution)/shard_map/ppermute | solution.py:40
  38.1 29.8 %collective-permute-start.9 = (bf16[272,640]{1,0:T(8,128)(2,1)S(1)}, bf16[272,640]{1,0:T(8,128)(2,1)S(1)}, u32[]{:S(2)}, u32[]{:S(2)}) collective-permute-start(bf16[272,640]{1,0:T(8,128)(2,1)S(1)} %shard_map.97.refs_4_), channel_id=1, source_target_pairs={{8,0},{0,8},{24,16},{16,24},{9,1},{1,9},{25,17},{17,25},{10,2},{2,... | collective-permute-start | bytes 1044488 | tf_op jit(solution)/shard_map/ppermute | solution.py:40
  38.2 30.6 %collective-permute-start.10 = (bf16[272,640]{1,0:T(8,128)(2,1)S(1)}, bf16[272,640]{1,0:T(8,128)(2,1)S(1)}, u32[]{:S(2)}, u32[]{:S(2)}) collective-permute-start(bf16[272,640]{1,0:T(8,128)(2,1)S(1)} %shard_map.97.refs_4_), channel_id=1, source_target_pairs={{16,0},{24,8},{0,16},{8,24},{17,1},{25,9},{1,17},{9,25},{18,2},{26... | collective-permute-start | bytes 1044488 | tf_op jit(solution)/shard_map/ppermute | solution.py:40
  40.2 30.8 %collective-permute-start.11 = (bf16[272,640]{1,0:T(8,128)(2,1)S(1)}, bf16[272,640]{1,0:T(8,128)(2,1)S(1)}, u32[]{:S(2)}, u32[]{:S(2)}) collective-permute-start(bf16[272,640]{1,0:T(8,128)(2,1)S(1)} %shard_map.97.refs_4_), channel_id=1, source_target_pairs={{24,0},{16,8},{8,16},{0,24},{25,1},{17,9},{9,17},{1,25},{26,2},{18... | collective-permute-start | bytes 1044488 | tf_op jit(solution)/shard_map/ppermute | solution.py:40
  43.9 18.0 %collective-permute-start.4 = (bf16[272,384]{1,0:T(8,128)(2,1)S(1)}, bf16[272,384]{1,0:T(8,128)(2,1)S(1)}, u32[]{:S(2)}, u32[]{:S(2)}) collective-permute-start(bf16[272,384]{1,0:T(8,128)(2,1)S(1)} %shard_map.96.refs_0_), channel_id=1, source_target_pairs={{16,0},{24,8},{0,16},{8,24},{17,1},{25,9},{1,17},{9,25},{18,2},{26... | collective-permute-start | bytes 626696 | tf_op jit(solution)/shard_map/ppermute | solution.py:40
  45.4 22.1 %collective-permute-start.5 = (bf16[272,384]{1,0:T(8,128)(2,1)S(1)}, bf16[272,384]{1,0:T(8,128)(2,1)S(1)}, u32[]{:S(2)}, u32[]{:S(2)}) collective-permute-start(bf16[272,384]{1,0:T(8,128)(2,1)S(1)} %shard_map.96.refs_0_), channel_id=1, source_target_pairs={{24,0},{16,8},{8,16},{0,24},{25,1},{17,9},{9,17},{1,25},{26,2},{18... | collective-permute-start | bytes 626696 | tf_op jit(solution)/shard_map/ppermute | solution.py:40
  62.0 23.3 %collective-permute-start.15 = (bf16[272,1024]{1,0:T(8,128)(2,1)S(1)}, bf16[272,1024]{1,0:T(8,128)(2,1)S(1)}, u32[]{:S(2)}, u32[]{:S(2)}) collective-permute-start(bf16[272,1024]{1,0:T(8,128)(2,1)S(1)} %get-tuple-element.18.refs_0_), channel_id=1, source_target_pairs={{6,0},{0,2},{2,4},{4,6},{7,1},{1,3},{3,5},{5,7},{14,8},{8,10},{10,... | collective-permute-start | bytes 1671176 | tf_op jit(solution)/shard_map/ppermute | solution.py:40
  67.5 17.7 %collective-permute-start.18 = (bf16[272,512]{1,0:T(8,128)(2,1)S(1)}, bf16[272,512]{1,0:T(8,128)(2,1)S(1)}, u32[]{:S(2)}, u32[]{:S(2)}) collective-permute-start(bf16[272,512]{1,0:T(8,128)(2,1)S(1)} %constant_dynamic-update-slice_fusion.refs_2_), channel_id=1, source_target_pairs={{8,0},{0,8},{24,16},{16,24},{9,1},{1,9},{25,17},{17,25},{10,2},{2,... | collective-permute-start | bytes 835592 | tf_op jit(solution)/shard_map/ppermute | solution.py:40
  67.9 17.3 %collective-permute-start.19 = (bf16[272,512]{1,0:T(8,128)(2,1)S(1)}, bf16[272,512]{1,0:T(8,128)(2,1)S(1)}, u32[]{:S(2)}, u32[]{:S(2)}) collective-permute-start(bf16[272,512]{1,0:T(8,128)(2,1)S(1)} %constant_dynamic-update-slice_fusion.refs_2_), channel_id=1, source_target_pairs={{16,0},{24,8},{0,16},{8,24},{17,1},{25,9},{1,17},{9,25},{18,2},{26... | collective-permute-start | bytes 835592 | tf_op jit(solution)/shard_map/ppermute | solution.py:40
  68.7 16.4 %collective-permute-start.20 = (bf16[272,512]{1,0:T(8,128)(2,1)S(1)}, bf16[272,512]{1,0:T(8,128)(2,1)S(1)}, u32[]{:S(2)}, u32[]{:S(2)}) collective-permute-start(bf16[272,512]{1,0:T(8,128)(2,1)S(1)} %constant_dynamic-update-slice_fusion.refs_2_), channel_id=1, source_target_pairs={{24,0},{16,8},{8,16},{0,24},{25,1},{17,9},{9,17},{1,25},{26,2},{18... | collective-permute-start | bytes 835592 | tf_op jit(solution)/shard_map/ppermute | solution.py:40
